TPU v7x, 32 devices: a whole 2x2x4 slice. The times are simulated.
32 devices in a mesh: dp: 8 (over y, x, core), seq: 4 (over z).
Axes of the slice: x: 2, y: 2, z: 4, core: 2. Of those that a mesh axis runs over, the one named last changes fastest.
Arguments:
- inputs: bfloat16 [24, 1024, 768], P('dp', 'seq'), may hold values from -6 to 6
- segment_ids: int32 [24, 1024], P('dp', 'seq'), may hold values from 0 to 3, never falling along the last dimension, each value on 1 to 512 neighbouring positions
- norm1_gain: bfloat16 [768], P('dp'), may hold values from 0.5 to 1.5
- norm1_shift: bfloat16 [768], P('dp'), may hold values from -1.5 to 1.5
- query_weight: bfloat16 [768, 768], P('dp'), may hold values from -0.4375 to 0.4375
- query_bias: bfloat16 [768], P('dp'), may hold values from -2.5 to 2.5
- key_weight: bfloat16 [768, 768], P('dp'), may hold values from -0.21875 to 0.21875
- value_weight: bfloat16 [768, 768], P('dp'), may hold values from -0.21875 to 0.21875
- value_bias: bfloat16 [768], P('dp'), may hold values from -1.5 to 1.5
- out_weight: bfloat16 [768, 768], P('dp'), may hold values from -0.625 to 0.625
- out_bias: bfloat16 [768], P('dp'), may hold values from -1.5 to 1.5
- norm2_gain: bfloat16 [768], P('dp'), may hold values from 0.5 to 1.5
- norm2_shift: bfloat16 [768], P('dp'), may hold values from -1.5 to 1.5
- fc1_weight: bfloat16 [768, 3072], P('dp'), may hold values from -0.21875 to 0.21875
- fc1_bias: bfloat16 [3072], P('dp'), may hold values from -1.5 to 1.5
- fc2_weight: bfloat16 [3072, 768], P('dp'), may hold values from -0.15625 to 0.15625
- fc2_bias: bfloat16 [768], P('dp'), may hold values from -1.5 to 1.5
- grad_output: bfloat16 [24, 1024, 768], P('dp', 'seq'), may hold values from -6 to 6
Outputs:
- output: bfloat16 [24, 1024, 768], P('dp', 'seq')
- grad_inputs: bfloat16 [24, 1024, 768], P('dp', 'seq')
- grad_norm1_gain: float32 [768], P('dp')
- grad_norm1_shift: float32 [768], P('dp')
- grad_query_weight: float32 [768, 768], P('dp')
- grad_query_bias: float32 [768], P('dp')
- grad_key_weight: float32 [768, 768], P('dp')
- grad_value_weight: float32 [768, 768], P('dp')
- grad_value_bias: float32 [768], P('dp')
- grad_out_weight: float32 [768, 768], P('dp')
- grad_out_bias: float32 [768], P('dp')
- grad_norm2_gain: float32 [768], P('dp')
- grad_norm2_shift: float32 [768], P('dp')
- grad_fc1_weight: float32 [768, 3072], P('dp')
- grad_fc1_bias: float32 [3072], P('dp')
- grad_fc2_weight: float32 [3072, 768], P('dp')
- grad_fc2_bias: float32 [768], P('dp')
Inputs may be any that keep to these rules, and one draw needn't show every extreme that they name: `segment_ids`: within each sequence, segment numbers never fall along the positions; each segment is a run of 1 to 512 positions.
All inputs are finite; a program needn't handle non-finite values.
Results may differ from a plain program's by a relative error of at most 0.017.
Values may be sent and summed in bfloat16 or wider, within the bound.
No kernel may reach another device: no remote copies, remote signals or barrier semaphores. Data moves between devices by JAX's collectives and lax.ppermute only.
A program may use at most 192 MiB of HBM per device.

v0:
```python
import jax
import jax.numpy as jnp
from jax import lax
from jax.sharding import PartitionSpec as P

HD = 64


EPSILON = 1e-05


def layer_norm(values, gain, shift):
    center = values - jnp.mean(values, axis=-1, keepdims=True)
    inverse = lax.rsqrt(jnp.mean(center * center, axis=-1, keepdims=True) + EPSILON)
    normed = center * inverse
    return (normed * gain + shift, normed, inverse)


def norm_back(grad, normed, inverse, gain):
    scaled = grad * gain
    return inverse * (
        scaled
        - jnp.mean(scaled, axis=-1, keepdims=True)
        - normed * jnp.mean(scaled * normed, axis=-1, keepdims=True)
    )


def gelu_slope(pre_act):
    return (
        0.5 * (1.0 + lax.erf(pre_act * 0.7071067811865476))
        + pre_act * jnp.exp(-0.5 * pre_act * pre_act) * 0.3989422804014327
    )


def cross_rows(left, right):
    return lax.dot_general(
        left, right, (((0,), (0,)), ((), ())), preferred_element_type=jnp.float32
    )


def times_transpose(left, right):
    return lax.dot_general(
        left, right, (((1,), (1,)), ((), ())), preferred_element_type=jnp.float32
    )


def to_pairs(array, heads_here):
    seqs_here, positions, _ = array.shape
    shaped = array.reshape(seqs_here, positions, heads_here, HD).transpose(0, 2, 1, 3)
    return shaped.reshape(seqs_here * heads_here, positions, HD)


def from_pairs(array, seqs_here, heads_here):
    positions = array.shape[1]
    shaped = array.reshape(seqs_here, heads_here, positions, HD).transpose(0, 2, 1, 3)
    return shaped.reshape(seqs_here, positions, heads_here * HD)


def masked_scores(query_pair, key_pair, segment_row):
    scores = jnp.einsum(
        "qd,kd->qk", query_pair, key_pair, preferred_element_type=jnp.float32
    ) * HD ** (-0.5)
    same_segment = segment_row[:, None] == segment_row[None, :]
    return jnp.where(same_segment, scores, -1e30)


def attend_forward(packed):
    query_pair, key_pair, value_pair, segment_row = packed
    scores = masked_scores(query_pair, key_pair, segment_row)
    highest = jnp.max(scores, axis=-1, keepdims=True)
    expon = jnp.exp(scores - highest)
    totals = jnp.sum(expon, axis=-1, keepdims=True)
    probs = (expon / totals).astype(jnp.bfloat16)
    result = jnp.dot(probs, value_pair, preferred_element_type=jnp.float32).astype(jnp.bfloat16)
    return (result, (highest + jnp.log(totals))[:, 0])


def attend_backward(packed):
    query_pair, key_pair, value_pair, segment_row, logsum, grad_pair = packed
    scores = masked_scores(query_pair, key_pair, segment_row)
    probs = jnp.exp(scores - logsum[:, None])
    grad_probs = jnp.einsum("qd,kd->qk", grad_pair, value_pair, preferred_element_type=jnp.float32)
    delta = jnp.sum(probs * grad_probs, axis=-1, keepdims=True)
    grad_scores = (probs * (grad_probs - delta)).astype(jnp.bfloat16)
    factor = HD ** (-0.5)
    grad_query = (
        jnp.einsum("qk,kd->qd", grad_scores, key_pair, preferred_element_type=jnp.float32) * factor
    ).astype(jnp.bfloat16)
    grad_key = (
        jnp.einsum("qk,qd->kd", grad_scores, query_pair, preferred_element_type=jnp.float32)
        * factor
    ).astype(jnp.bfloat16)
    grad_value = jnp.einsum(
        "qk,qd->kd", probs.astype(jnp.bfloat16), grad_pair, preferred_element_type=jnp.float32
    ).astype(jnp.bfloat16)
    return (grad_query, grad_key, grad_value)


def column_sum(array):
    return jnp.sum(array.astype(jnp.float32), axis=0)


def per_device(
    inputs,
    segment_ids,
    norm1_gain,
    norm1_shift,
    query_weight,
    query_bias,
    key_weight,
    value_weight,
    value_bias,
    out_weight,
    out_bias,
    norm2_gain,
    norm2_shift,
    fc1_weight,
    fc1_bias,
    fc2_weight,
    fc2_bias,
    grad_output,
):
    seqs_here, positions, model_width = inputs.shape
    token_rows = seqs_here * positions
    (
        first_gain,
        first_shift,
        w_query,
        b_query,
        w_key,
        w_value,
        b_value,
        w_out,
        b_out,
        second_gain,
        second_shift,
        w_up,
        b_up,
        w_down,
        b_down,
    ) = (
        lax.all_gather(norm1_gain, "dp", axis=0, tiled=True),
        lax.all_gather(norm1_shift, "dp", axis=0, tiled=True),
        lax.all_gather(query_weight, "dp", axis=0, tiled=True),
        lax.all_gather(query_bias, "dp", axis=0, tiled=True),
        lax.all_gather(key_weight, "dp", axis=0, tiled=True),
        lax.all_gather(value_weight, "dp", axis=0, tiled=True),
        lax.all_gather(value_bias, "dp", axis=0, tiled=True),
        lax.all_gather(out_weight, "dp", axis=0, tiled=True),
        lax.all_gather(out_bias, "dp", axis=0, tiled=True),
        lax.all_gather(norm2_gain, "dp", axis=0, tiled=True),
        lax.all_gather(norm2_shift, "dp", axis=0, tiled=True),
        lax.all_gather(fc1_weight, "dp", axis=0, tiled=True),
        lax.all_gather(fc1_bias, "dp", axis=0, tiled=True),
        lax.all_gather(fc2_weight, "dp", axis=0, tiled=True),
        lax.all_gather(fc2_bias, "dp", axis=0, tiled=True),
    )
    full_segments = lax.all_gather(segment_ids, "seq", axis=1, tiled=True)
    flat_in = inputs.reshape(token_rows, model_width).astype(jnp.float32)
    normed_one, unit_one, inverse_one = layer_norm(
        flat_in, first_gain.astype(jnp.float32), first_shift.astype(jnp.float32)
    )
    act_one = normed_one.astype(jnp.bfloat16)
    query_tok = (
        jnp.dot(act_one, w_query, preferred_element_type=jnp.float32) + b_query.astype(jnp.float32)
    ).astype(jnp.bfloat16)
    key_tok = jnp.dot(act_one, w_key, preferred_element_type=jnp.float32).astype(jnp.bfloat16)
    value_tok = (
        jnp.dot(act_one, w_value, preferred_element_type=jnp.float32) + b_value.astype(jnp.float32)
    ).astype(jnp.bfloat16)
    query_heads, key_heads, value_heads = (
        lax.all_to_all(
            query_tok.reshape(seqs_here, positions, model_width),
            "seq",
            split_axis=2,
            concat_axis=1,
            tiled=True,
        ),
        lax.all_to_all(
            key_tok.reshape(seqs_here, positions, model_width),
            "seq",
            split_axis=2,
            concat_axis=1,
            tiled=True,
        ),
        lax.all_to_all(
            value_tok.reshape(seqs_here, positions, model_width),
            "seq",
            split_axis=2,
            concat_axis=1,
            tiled=True,
        ),
    )
    heads_here = query_heads.shape[2] // HD
    query_pairs = to_pairs(query_heads, heads_here)
    key_pairs = to_pairs(key_heads, heads_here)
    value_pairs = to_pairs(value_heads, heads_here)
    segment_pairs = jnp.repeat(full_segments, heads_here, axis=0)
    attn_pairs, logsum = lax.map(
        attend_forward, (query_pairs, key_pairs, value_pairs, segment_pairs)
    )
    attn_heads = from_pairs(attn_pairs, seqs_here, heads_here)
    attn_tok = lax.all_to_all(attn_heads, "seq", split_axis=1, concat_axis=2, tiled=True).reshape(
        token_rows, model_width
    )
    middle = (
        flat_in
        + jnp.dot(attn_tok, w_out, preferred_element_type=jnp.float32)
        + b_out.astype(jnp.float32)
    )
    normed_two, unit_two, inverse_two = layer_norm(
        middle, second_gain.astype(jnp.float32), second_shift.astype(jnp.float32)
    )
    act_two = normed_two.astype(jnp.bfloat16)
    pre_act = jnp.dot(act_two, w_up, preferred_element_type=jnp.float32) + b_up.astype(jnp.float32)
    hidden = jax.nn.gelu(pre_act, approximate=False).astype(jnp.bfloat16)
    result = (
        middle
        + jnp.dot(hidden, w_down, preferred_element_type=jnp.float32)
        + b_down.astype(jnp.float32)
    )
    output = result.astype(jnp.bfloat16).reshape(seqs_here, positions, model_width)
    first_gain_b, w_query_b, w_key_b, w_value_b, w_out_b, second_gain_b, w_up_b, w_down_b = (
        lax.all_gather(norm1_gain, "dp", axis=0, tiled=True),
        lax.all_gather(query_weight, "dp", axis=0, tiled=True),
        lax.all_gather(key_weight, "dp", axis=0, tiled=True),
        lax.all_gather(value_weight, "dp", axis=0, tiled=True),
        lax.all_gather(out_weight, "dp", axis=0, tiled=True),
        lax.all_gather(norm2_gain, "dp", axis=0, tiled=True),
        lax.all_gather(fc1_weight, "dp", axis=0, tiled=True),
        lax.all_gather(fc2_weight, "dp", axis=0, tiled=True),
    )
    grad_down = grad_output.reshape(token_rows, model_width)
    d_b_down = column_sum(grad_down)
    d_w_down = cross_rows(hidden, grad_down)
    grad_hidden = times_transpose(grad_down, w_down_b)
    grad_pre = (grad_hidden * gelu_slope(pre_act)).astype(jnp.bfloat16)
    d_b_up = column_sum(grad_pre)
    d_w_up = cross_rows(act_two, grad_pre)
    grad_two = times_transpose(grad_pre, w_up_b)
    d_second_gain = jnp.sum(grad_two * unit_two, axis=0)
    d_second_shift = jnp.sum(grad_two, axis=0)
    grad_middle = grad_down.astype(jnp.float32) + norm_back(
        grad_two, unit_two, inverse_two, second_gain_b.astype(jnp.float32)
    )
    grad_branch = grad_middle.astype(jnp.bfloat16)
    d_b_out = column_sum(grad_branch)
    d_w_out = cross_rows(attn_tok, grad_branch)
    grad_attn = (
        times_transpose(grad_branch, w_out_b)
        .astype(jnp.bfloat16)
        .reshape(seqs_here, positions, model_width)
    )
    grad_attn_heads = lax.all_to_all(grad_attn, "seq", split_axis=2, concat_axis=1, tiled=True)
    grad_query_pairs, grad_key_pairs, grad_value_pairs = lax.map(
        attend_backward,
        (
            query_pairs,
            key_pairs,
            value_pairs,
            segment_pairs,
            logsum,
            to_pairs(grad_attn_heads, heads_here),
        ),
    )
    grad_query_tok, grad_key_tok, grad_value_tok = (
        lax.all_to_all(
            from_pairs(grad_query_pairs, seqs_here, heads_here),
            "seq",
            split_axis=1,
            concat_axis=2,
            tiled=True,
        ),
        lax.all_to_all(
            from_pairs(grad_key_pairs, seqs_here, heads_here),
            "seq",
            split_axis=1,
            concat_axis=2,
            tiled=True,
        ),
        lax.all_to_all(
            from_pairs(grad_value_pairs, seqs_here, heads_here),
            "seq",
            split_axis=1,
            concat_axis=2,
            tiled=True,
        ),
    )
    grad_query_tok = grad_query_tok.reshape(token_rows, model_width)
    grad_key_tok = grad_key_tok.reshape(token_rows, model_width)
    grad_value_tok = grad_value_tok.reshape(token_rows, model_width)
    d_b_query = column_sum(grad_query_tok)
    d_b_value = column_sum(grad_value_tok)
    d_w_query = cross_rows(act_one, grad_query_tok)
    d_w_key = cross_rows(act_one, grad_key_tok)
    d_w_value = cross_rows(act_one, grad_value_tok)
    grad_one = (
        times_transpose(grad_query_tok, w_query_b)
        + times_transpose(grad_key_tok, w_key_b)
        + times_transpose(grad_value_tok, w_value_b)
    )
    d_first_gain = jnp.sum(grad_one * unit_one, axis=0)
    d_first_shift = jnp.sum(grad_one, axis=0)
    grad_inputs = grad_middle + norm_back(
        grad_one, unit_one, inverse_one, first_gain_b.astype(jnp.float32)
    )
    grad_inputs = grad_inputs.astype(jnp.bfloat16).reshape(seqs_here, positions, model_width)
    (
        part_first_gain,
        part_first_shift,
        part_w_query,
        part_b_query,
        part_w_key,
        part_w_value,
        part_b_value,
        part_w_out,
        part_b_out,
        part_second_gain,
        part_second_shift,
        part_w_up,
        part_b_up,
        part_w_down,
        part_b_down,
    ) = (
        lax.psum_scatter(d_first_gain, "dp", scatter_dimension=0, tiled=True),
        lax.psum_scatter(d_first_shift, "dp", scatter_dimension=0, tiled=True),
        lax.psum_scatter(d_w_query, "dp", scatter_dimension=0, tiled=True),
        lax.psum_scatter(d_b_query, "dp", scatter_dimension=0, tiled=True),
        lax.psum_scatter(d_w_key, "dp", scatter_dimension=0, tiled=True),
        lax.psum_scatter(d_w_value, "dp", scatter_dimension=0, tiled=True),
        lax.psum_scatter(d_b_value, "dp", scatter_dimension=0, tiled=True),
        lax.psum_scatter(d_w_out, "dp", scatter_dimension=0, tiled=True),
        lax.psum_scatter(d_b_out, "dp", scatter_dimension=0, tiled=True),
        lax.psum_scatter(d_second_gain, "dp", scatter_dimension=0, tiled=True),
        lax.psum_scatter(d_second_shift, "dp", scatter_dimension=0, tiled=True),
        lax.psum_scatter(d_w_up, "dp", scatter_dimension=0, tiled=True),
        lax.psum_scatter(d_b_up, "dp", scatter_dimension=0, tiled=True),
        lax.psum_scatter(d_w_down, "dp", scatter_dimension=0, tiled=True),
        lax.psum_scatter(d_b_down, "dp", scatter_dimension=0, tiled=True),
    )
    (
        shard_first_gain,
        shard_first_shift,
        shard_w_query,
        shard_b_query,
        shard_w_key,
        shard_w_value,
        shard_b_value,
        shard_w_out,
        shard_b_out,
        shard_second_gain,
        shard_second_shift,
        shard_w_up,
        shard_b_up,
        shard_w_down,
        shard_b_down,
    ) = (
        lax.psum(part_first_gain.astype(jnp.bfloat16), "seq").astype(jnp.float32),
        lax.psum(part_first_shift.astype(jnp.bfloat16), "seq").astype(jnp.float32),
        lax.psum(part_w_query.astype(jnp.bfloat16), "seq").astype(jnp.float32),
        lax.psum(part_b_query.astype(jnp.bfloat16), "seq").astype(jnp.float32),
        lax.psum(part_w_key.astype(jnp.bfloat16), "seq").astype(jnp.float32),
        lax.psum(part_w_value.astype(jnp.bfloat16), "seq").astype(jnp.float32),
        lax.psum(part_b_value.astype(jnp.bfloat16), "seq").astype(jnp.float32),
        lax.psum(part_w_out.astype(jnp.bfloat16), "seq").astype(jnp.float32),
        lax.psum(part_b_out.astype(jnp.bfloat16), "seq").astype(jnp.float32),
        lax.psum(part_second_gain.astype(jnp.bfloat16), "seq").astype(jnp.float32),
        lax.psum(part_second_shift.astype(jnp.bfloat16), "seq").astype(jnp.float32),
        lax.psum(part_w_up.astype(jnp.bfloat16), "seq").astype(jnp.float32),
        lax.psum(part_b_up.astype(jnp.bfloat16), "seq").astype(jnp.float32),
        lax.psum(part_w_down.astype(jnp.bfloat16), "seq").astype(jnp.float32),
        lax.psum(part_b_down.astype(jnp.bfloat16), "seq").astype(jnp.float32),
    )
    return (
        output,
        grad_inputs,
        shard_first_gain,
        shard_first_shift,
        shard_w_query,
        shard_b_query,
        shard_w_key,
        shard_w_value,
        shard_b_value,
        shard_w_out,
        shard_b_out,
        shard_second_gain,
        shard_second_shift,
        shard_w_up,
        shard_b_up,
        shard_w_down,
        shard_b_down,
    )


def solution(mesh):
    placed = (
        P("dp", "seq", None),
        P("dp", "seq"),
        P("dp"),
        P("dp"),
        P("dp", None),
        P("dp"),
        P("dp", None),
        P("dp", None),
        P("dp"),
        P("dp", None),
        P("dp"),
        P("dp"),
        P("dp"),
        P("dp", None),
        P("dp"),
        P("dp", None),
        P("dp"),
        P("dp", "seq", None),
    )
    return jax.shard_map(
        per_device,
        mesh=mesh,
        in_specs=placed,
        out_specs=(
            P("dp", "seq", None),
            P("dp", "seq", None),
            P("dp"),
            P("dp"),
            P("dp", None),
            P("dp"),
            P("dp", None),
            P("dp", None),
            P("dp"),
            P("dp", None),
            P("dp"),
            P("dp"),
            P("dp"),
            P("dp", None),
            P("dp"),
            P("dp", None),
            P("dp"),
        ),
        check_vma=False,
    )
```

profile of v0, /device:TPU:0, one launch (start us, length us, event | category | flops | bytes accessed | tf_op | source)
XLA Modules:
  0.0 1093.3 jit_solution(9284306337476619404)
XLA Ops:
  15.2 26.3 %all-reduce.18 = (bf16[768]{0:T(1024)(128)(2,1)S(1)}, bf16[768]{0:T(1024)(128)(2,1)S(1)}, bf16[768]{0:T(1024)(128)(2,1)S(1)}, bf16[768]{0:T(1024)(128)(2,1)S(1)}...) all-reduce(bf16[768]{0:T(1024)(128)(2,1)S(1)} %dynamic-update-slice, ...), channel_id=1, replica_groups=mesh['dp'=8,'seq'=4] {'dp'}, use_global_device_ids=true, to_apply=%add.1 | all-reduce | flops 6144 | bytes 24576
  47.7 5.0 all-to-all-start
  53.4 9.6 all-gather.12.cloned.1.call-done
  70.2 16.2 %all-to-all-done = bf16[3,256,768]{1,0,2:T(4,128)(2,1)S(1)} async-done(((bf16[3,256,768]{1,0,2:T(4,128)(2,1)}), bf16[3,256,768]{1,0,2:T(4,128)(2,1)S(1)}, u32[]{:S(2)}, u32[]{:S(2)}) %all-to-all-start) | async-done | bytes 1179680 | tf_op jit(solution)/shard_map/all_to_all | solution.py:172
  86.5 4.3 all-to-all-start.2
  98.7 28.6 %all-to-all-done.2 = bf16[3,256,768]{1,0,2:T(4,128)(2,1)} async-done(((bf16[3,256,768]{1,0,2:T(4,128)(2,1)}), bf16[3,256,768]{1,0,2:T(4,128)(2,1)}, u32[]{:S(2)}, u32[]{:S(2)}) %all-to-all-start.2) | async-done | bytes 1179680 | tf_op jit(solution)/shard_map/all_to_all | solution.py:186
  127.3 4.3 all-to-all-start.1
  132.3 41.2 %all_gather.56 = s32[3,1024]{1,0:T(4,128)S(1)} all-gather(s32[3,256]{1,0:T(4,128)S(1)} %copy-done.26), channel_id=1, replica_groups=mesh['dp'=8,'seq'=4] {'seq'}, dimensions={1}, use_global_device_ids=true | all-gather | bytes 15360 | tf_op jit(solution)/shard_map/all_gather | solution.py:158
  202.1 99.2 %while.26 = (s32[]{:T(128)}, bf16[9,1024,64]{1,2,0:T(8,128)(2,1)}, f32[9,1024]{1,0:T(8,128)}, s32[9,1024]{1,0:T(8,128)}, bf16[9,1024,64]{2,1,0:T(8,128)(2,1)S(1)...) while((s32[]{:T(128)}, bf16[9,1024,64]{1,2,0:T(8,128)(2,1)}, ...), condition=%wide.region_5.6_spmd, body=%wide.region_2.5_spmd.sunk | while | flops 284228608 | bytes 30349440 | solution.py:199
  208.9 4.2 fusion.156
  219.9 4.2 fusion.156
  230.9 4.2 fusion.156
  242.0 4.2 fusion.156
  253.0 4.2 fusion.156
  264.0 4.2 fusion.156
  275.0 4.2 fusion.156
  286.0 4.2 fusion.156
  297.1 4.2 fusion.156
  301.3 4.2 copy.112
  305.5 4.6 all-to-all-start.3
  311.4 10.1 all-gather
  322.2 33.6 %all-to-all-done.3 = bf16[3,1024,192]{2,0,1:T(4,128)(2,1)} async-done(((bf16[3,1024,192]{2,0,1:T(4,128)(2,1)}), bf16[3,1024,192]{2,0,1:T(4,128)(2,1)}, u32[]{:S(2)}, u32[]{:S(2)}) %all-to-all-start.3) | async-done | bytes 1179680 | tf_op jit(solution)/shard_map/all_to_all | solution.py:203
  364.3 27.2 %fusion.56 = (bf16[768,3072]{1,0:T(8,128)(2,1)}, f32[768,3072]{1,0:T(8,128)}) fusion(f32[3072]{0:T(1024)} %bitcast.275, bf16[768,3072]{1,0:T(8,128)(2,1)} %all-gather.16.cloned.1.call-done, f32[768,768]{1,0:T(8,128)S(1)} %get-tuple-element.265, f32[768]{0:T(1024)S(1)} %convert_element_type.227, f32[768]{0:T(1024)S(1)} %convert_element_type.226, ...), kind=kOutput, calls=%fused_computation.64 | convolution fusion | flops 3782541312 | bytes 21258240 | tf_op jit(solution)/shard_map/dot_general | solution.py:215
  391.5 11.8 %convert_reduce_fusion = (f32[3072]{0:T(1024)}, bf16[768,3072]{1,0:T(8,128)(2,1)S(1)}) fusion(f32[768,3072]{1,0:T(8,128)} %get-tuple-element.267, f32[3072]{0:T(1024)} %bitcast.276, bf16[768,768]{1,0:T(8,128)(2,1)} %bitcast.249, bf16[3072,768]{1,0:T(8,128)(2,1)} %all-gather.18.cloned.1.call-done), kind=kOutput, calls=%fused_computation.71 | convolution fusion | flops 3654546432 | bytes 20078592 | tf_op jit(solution)/shard_map/dot_general | solution.py:42
  403.4 4.8 multiply_reduce_fusion.1
  415.6 4.3 all-to-all-start.4
  420.0 4.5 fusion.90
  424.6 31.9 %all-to-all-done.4 = bf16[3,256,768]{1,0,2:T(4,128)(2,1)} async-done(((bf16[3,256,768]{1,0,2:T(4,128)(2,1)}), bf16[3,256,768]{1,0,2:T(4,128)(2,1)}, u32[]{:S(2)}, u32[]{:S(2)}) %all-to-all-start.4) | async-done | bytes 1179680 | tf_op jit(solution)/shard_map/all_to_all | solution.py:254
  467.0 124.1 %while.27 = (s32[]{:T(128)}, bf16[9,1024,64]{1,2,0:T(8,128)(2,1)}, bf16[9,1024,64]{1,2,0:T(8,128)(2,1)}, bf16[9,1024,64]{1,2,0:T(8,128)(2,1)}, s32[9,1024]{1,0:T...) while((s32[]{:T(128)}, bf16[9,1024,64]{1,2,0:T(8,128)(2,1)}, ...), condition=%wide.region_12.13_spmd, body=%wide.region_10.12_spmd.sunk | while | flops 681901056 | bytes 33465460 | solution.py:255
  595.3 4.4 all-to-all-start.5
  602.0 45.5 %all-to-all-done.5 = bf16[3,1024,192]{2,0,1:T(4,128)(2,1)} async-done(((bf16[3,1024,192]{2,0,1:T(4,128)(2,1)}), bf16[3,1024,192]{2,0,1:T(4,128)(2,1)}, u32[]{:S(2)}, u32[]{:S(2)}) %all-to-all-start.5) | async-done | bytes 1179680 | tf_op jit(solution)/shard_map/all_to_all | solution.py:267
  647.4 4.2 copy.124
  655.7 4.2 fusion.99
  659.9 4.1 copy.125
  664.0 51.5 %all_to_all.120 = bf16[3,1024,192]{2,0,1:T(4,128)(2,1)S(1)} all-to-all(bf16[3,1024,192]{2,0,1:T(4,128)(2,1)} %copy.125), channel_id=1, replica_groups=mesh['dp'=8,'seq'=4] {'seq'}, dimensions={1} | all-to-all | bytes 2359296 | tf_op jit(solution)/shard_map/all_to_all | solution.py:274
  722.1 4.2 fusion.100
  730.5 50.8 %all_to_all.121 = bf16[3,1024,192]{2,0,1:T(4,128)(2,1)S(1)} all-to-all(bf16[3,1024,192]{2,0,1:T(4,128)(2,1)} %copy.128), channel_id=1, replica_groups=mesh['dp'=8,'seq'=4] {'seq'}, dimensions={1} | all-to-all | bytes 2359296 | tf_op jit(solution)/shard_map/all_to_all | solution.py:281
  789.3 4.1 fusion.101
  793.5 9.0 fusion.93
  802.6 10.6 fusion.102
  817.2 8.6 add_convert_fusion
  825.8 4.4 copy.135
  839.9 4.1 fusion.97
  849.0 67.8 %reduce-scatter.15.cloned.1.call-done = f32[96,3072]{1,0:T(8,128)} async-done(((f32[768,3072]{1,0:T(8,128)}), f32[96,3072]{1,0:T(8,128)}) %reduce-scatter.15.cloned.1.call-update) | async-done | bytes 1179664 | tf_op jit(solution)/shard_map/reduce_scatter | solution.py:336
  919.0 77.7 %reduce-scatter.17.cloned.1.call-done = f32[384,768]{1,0:T(8,128)} async-done(((f32[3072,768]{1,0:T(8,128)}), f32[384,768]{1,0:T(8,128)}) %reduce-scatter.17.cloned.1.call-update) | async-done | bytes 1179664 | tf_op jit(solution)/shard_map/reduce_scatter | solution.py:338
  1005.2 26.3 %all-reduce.17 = (bf16[768]{0:T(1024)(128)(2,1)}, bf16[768]{0:T(1024)(128)(2,1)}, bf16[768]{0:T(1024)(128)(2,1)}, bf16[768]{0:T(1024)(128)(2,1)}, bf16[768]{0:T(...) all-reduce(f32[768]{0:T(1024)} %get-tuple-element.184, ...), channel_id=2, replica_groups=mesh['dp'=8,'seq'=4] {'dp'}, use_global_device_ids=true, to_apply=%region_16.17.clone | all-reduce | flops 9216 | bytes 55296
  1042.2 13.1 %all-reduce.19 = (bf16[96]{0:T(256)(128)(2,1)}, bf16[96]{0:T(256)(128)(2,1)}, bf16[96]{0:T(256)(128)(2,1)}, bf16[96]{0:T(256)(128)(2,1)}, bf16[96]{0:T(256)(128)...) all-reduce(bf16[96]{0:T(256)(128)(2,1)} %dynamic-slice.43, ...), channel_id=1, replica_groups=mesh['dp'=8,'seq'=4] {'seq'}, use_global_device_ids=true, to_apply=%region_17.18 | all-reduce | flops 1152 | bytes 4608 | tf_op jit(solution)/shard_map/psum | solution.py:358
  1070.8 8.2 all-reduce.23.cloned.1.call-done
  (382 shorter events, 362.7 us)
Async XLA Ops:
  7.2 4.9 copy-start.31
  7.2 34.9 %copy-start.1 = (bf16[3,256,768]{2,1,0:T(8,128)(2,1)S(1)}, bf16[3,256,768]{2,1,0:T(8,128)(2,1)}, u32[]{:S(2)}) copy-start(bf16[3,256,768]{2,1,0:T(8,128)(2,1)} %param.22) | copy-start | bytes 3538948
  7.2 6.1 copy-start.36
  7.2 6.4 copy-start.37
  7.2 6.6 copy-start.38
  7.2 6.8 copy-start.39
  7.3 7.0 copy-start.40
  7.3 7.3 copy-start.41
  7.3 7.5 copy-start.42
  7.3 7.7 copy-start.43
  7.3 35.4 %all-gather.8.cloned.1.call-start = ((), (), s32[]{:S(2)}) async-start(), calls=%async_computation.14 | async-start | bytes 1327104 | tf_op jit(solution)/shard_map/all_gather | solution.py:144
  8.0 54.9 %all-gather.12.cloned.1.call-start = ((), (), s32[]{:S(2)}) async-start(), calls=%async_computation.16 | async-start | bytes 1327104 | tf_op jit(solution)/shard_map/all_gather | solution.py:147
  10.3 31.3 %copy-start.18 = (f32[3,256]{1,0:T(4,128)}, f32[3,256]{1,0:T(4,128)S(1)}, u32[]{:S(2)}) copy-start(f32[3,256]{1,0:T(4,128)S(1)} %broadcast_multiply_fusion.5) | copy-start | bytes 9220
  12.1 30.6 %copy-start.19 = (f32[768]{0:T(1024)}, f32[768]{0:T(1024)S(1)}, u32[]{:S(2)}) copy-start(f32[768]{0:T(1024)S(1)} %div.35) | copy-start | bytes 9220
  47.7 38.8 %all-to-all-start = ((bf16[3,256,768]{1,0,2:T(4,128)(2,1)}), bf16[3,256,768]{1,0,2:T(4,128)(2,1)S(1)}, u32[]{:S(2)}, u32[]{:S(2)}) async-start(bf16[3,256,768]{1,0,2:T(4,128)(2,1)} %copy.100), calls=%async_computation | async-start | bytes 3145728 | tf_op jit(solution)/shard_map/all_to_all | solution.py:172
  52.6 38.8 %all-gather.10.cloned.1.call-start = ((), (), s32[]{:S(2)}) async-start(), calls=%async_computation.15 | async-start | bytes 1327104 | tf_op jit(solution)/shard_map/all_gather | solution.py:146
  86.5 40.9 %all-to-all-start.2 = ((bf16[3,256,768]{1,0,2:T(4,128)(2,1)}), bf16[3,256,768]{1,0,2:T(4,128)(2,1)}, u32[]{:S(2)}, u32[]{:S(2)}) async-start(bf16[3,256,768]{1,0,2:T(4,128)(2,1)} %copy.106), calls=%async_computation.2 | async-start | bytes 3145728 | tf_op jit(solution)/shard_map/all_to_all | solution.py:186
  90.8 270.2 %all-gather.14.cloned.1.call-start = ((), (), s32[]{:S(2)}) async-start(), calls=%async_computation.17 | async-start | bytes 1327104 | tf_op jit(solution)/shard_map/all_gather | solution.py:149
  98.7 33.6 %copy-start.26 = (s32[3,256]{1,0:T(4,128)S(1)}, s32[3,256]{1,0:T(4,128)}, u32[]{:S(2)}) copy-start(s32[3,256]{1,0:T(4,128)} %param.23) | copy-start | bytes 9220
  127.3 63.0 %all-to-all-start.1 = ((bf16[3,256,768]{1,0,2:T(4,128)(2,1)}), bf16[3,256,768]{1,0,2:T(4,128)(2,1)}, u32[]{:S(2)}, u32[]{:S(2)}) async-start(bf16[3,256,768]{1,0,2:T(4,128)(2,1)} %copy.103), calls=%async_computation.1 | async-start | bytes 3145728 | tf_op jit(solution)/shard_map/all_to_all | solution.py:179
  131.7 232.6 %all-gather.16.cloned.1.call-start = ((), (), s32[]{:S(2)}) async-start(), calls=%async_computation.18 | async-start | bytes 5308416 | tf_op jit(solution)/shard_map/all_gather | solution.py:153
  301.2 4.3 copy-start.4
  305.5 5.2 copy-start.30
  305.5 5.2 copy-start.29
  305.5 5.2 copy-start.28
  305.5 50.2 %all-to-all-start.3 = ((bf16[3,1024,192]{2,0,1:T(4,128)(2,1)}), bf16[3,1024,192]{2,0,1:T(4,128)(2,1)}, u32[]{:S(2)}, u32[]{:S(2)}) async-start(bf16[3,1024,192]{2,0,1:T(4,128)(2,1)} %copy.112), calls=%async_computation.3 | async-start | bytes 4194304 | tf_op jit(solution)/shard_map/all_to_all | solution.py:203
  310.1 81.4 %all-gather.18.cloned.1.call-start = ((), (), s32[]{:S(2)}) async-start(), calls=%async_computation.19 | async-start | bytes 5308416 | tf_op jit(solution)/shard_map/all_gather | solution.py:155
  391.5 11.8 %copy-start.32 = (bf16[768,3072]{1,0:T(8,128)(2,1)S(1)}, bf16[768,3072]{1,0:T(8,128)(2,1)}, u32[]{:S(2)}) copy-start(bf16[768,3072]{1,0:T(8,128)(2,1)} %all-gather.16.cloned.1.call-done) | copy-start | bytes 14155780
  403.4 4.8 copy-start.8
  403.4 4.8 copy-start.7
  415.6 40.9 %all-to-all-start.4 = ((bf16[3,256,768]{1,0,2:T(4,128)(2,1)}), bf16[3,256,768]{1,0,2:T(4,128)(2,1)}, u32[]{:S(2)}, u32[]{:S(2)}) async-start(bf16[3,256,768]{1,0,2:T(4,128)(2,1)} %copy.115), calls=%async_computation.4 | async-start | bytes 3145728 | tf_op jit(solution)/shard_map/all_to_all | solution.py:254
  420.0 418.3 %reduce-scatter.13.cloned.1.call-start = ((), (), s32[]{:S(2)}) async-start(), calls=%async_computation.23 | async-start | bytes 2654208 | tf_op jit(solution)/shard_map/reduce_scatter | solution.py:332
  595.3 52.2 %all-to-all-start.5 = ((bf16[3,1024,192]{2,0,1:T(4,128)(2,1)}), bf16[3,1024,192]{2,0,1:T(4,128)(2,1)}, u32[]{:S(2)}, u32[]{:S(2)}) async-start(bf16[3,1024,192]{2,0,1:T(4,128)(2,1)} %copy.122), calls=%async_computation.5 | async-start | bytes 4194304 | tf_op jit(solution)/shard_map/all_to_all | solution.py:267
  599.7 244.4 %reduce-scatter.7.cloned.1.call-start = ((), (), s32[]{:S(2)}) async-start(), calls=%async_computation.20 | async-start | bytes 2654208 | tf_op jit(solution)/shard_map/reduce_scatter | solution.py:327
  659.9 185.8 %reduce-scatter.9.cloned.1.call-start = ((), (), s32[]{:S(2)}) async-start(), calls=%async_computation.21 | async-start | bytes 2654208 | tf_op jit(solution)/shard_map/reduce_scatter | solution.py:329
  726.4 121.0 %reduce-scatter.11.cloned.1.call-start = ((), (), s32[]{:S(2)}) async-start(), calls=%async_computation.22 | async-start | bytes 2654208 | tf_op jit(solution)/shard_map/reduce_scatter | solution.py:330
  793.5 123.4 %reduce-scatter.15.cloned.1.call-start = ((), (), s32[]{:S(2)}) async-start(), calls=%async_computation.24 | async-start | bytes 10616832 | tf_op jit(solution)/shard_map/reduce_scatter | solution.py:336
  802.5 194.2 %reduce-scatter.17.cloned.1.call-start = ((), (), s32[]{:S(2)}) async-start(), calls=%async_computation.25 | async-start | bytes 10616832 | tf_op jit(solution)/shard_map/reduce_scatter | solution.py:338
  813.2 265.8 %all-reduce.23.cloned.1.call-start = ((), (), s32[]{:S(2)}) async-start(), calls=%async_computation.26 | async-start | bytes 3538944 | tf_op jit(solution)/shard_map/psum | solution.py:360
  825.8 7.0 copy-start.3
  849.0 149.9 %copy-start.10 = (bf16[768,768]{1,0:T(8,128)(2,1)S(1)}, bf16[768,768]{1,0:T(8,128)(2,1)}, u32[]{:S(2)}) copy-start(bf16[768,768]{1,0:T(8,128)(2,1)} %reshape.310) | copy-start | bytes 3538948
  849.0 149.9 %copy-start.34 = (bf16[768,768]{1,0:T(8,128)(2,1)S(1)}, bf16[768,768]{1,0:T(8,128)(2,1)}, u32[]{:S(2)}) copy-start(bf16[768,768]{1,0:T(8,128)(2,1)} %all-gather.10.cloned.1.call-done) | copy-start | bytes 3538948
  1001.3 3.8 copy-start.25
  1001.3 65.9 %copy-start.6 = (f32[768,768]{1,0:T(8,128)S(1)}, f32[768,768]{1,0:T(8,128)}, u32[]{:S(2)}) copy-start(f32[768,768]{1,0:T(8,128)} %copy-done.5) | copy-start | bytes 7077892
  1079.0 4.4 copy-start.15
  1079.0 5.1 copy-start.14
  1079.0 5.9 copy-start.13
  1079.0 6.6 copy-start.12
  (24 other events, 40.0 us)
Sparse Core Ops, SparseCore 0:
  10.0 26.8 all-gather.7
  38.8 24.0 all-gather.11
  64.8 24.0 all-gather.9
  93.2 26.1 all-gather.13
  134.1 41.8 all-gather.15
  312.5 41.8 all-gather.17
  424.7 45.4 reduce-scatter.12
  660.0 43.1 reduce-scatter.6
  726.5 43.1 reduce-scatter.8
  793.6 43.2 reduce-scatter.10
  840.4 76.4 reduce-scatter.14
  920.2 76.4 reduce-scatter.16
  1000.7 78.2 all-reduce.22
where the time goes:
time: 1110 us; the launch traced here: 1090 us
  waiting for transfers between devices  323 us (29%)
  matrix products  266 us (24%)
  blocking collectives  219 us (20%)
  local copies, waits for them, and re-layouts  172 us (15%)
  other arithmetic  68 us (6%)
  starting transfers between devices  27.8 us (3%)
  between operations  16.9 us (2%)
    reduce_scatter x1, waiting for transfers between devices, per_device(): lax.psum_scatter(d_w_down, 'dp', scatter_dimension=0, tiled=True)  77.7 us
    reduce_scatter x1, waiting for transfers between devices, per_device(): lax.psum_scatter(d_w_up, 'dp', scatter_dimension=0, tiled=True)  67.8 us
    unnamed x2, blocking collectives  52.5 us
    all_to_all x1, blocking collectives, per_device(): lax.all_to_all(from_pairs(grad_key_pairs, seqs_here, heads_here), 'seq',...  51.5 us
    all_to_all x1, blocking collectives, per_device(): lax.all_to_all(from_pairs(grad_value_pairs, seqs_here, heads_here), 'seq'...  50.8 us
    all_to_all x1, waiting for transfers between devices, per_device(): lax.all_to_all(from_pairs(grad_query_pairs, seqs_here, heads_here), 'seq'...  45.5 us
    all_gather x1, blocking collectives, per_device(): full_segments = lax.all_gather(segment_ids, 'seq', axis=1, tiled=True)  41.2 us
    dot_general x18, matrix products, masked_scores(): jnp.einsum('qd,kd->qk', query_pair, key_pair, preferred_element_type=jnp....  38.3 us
  transfers between devices with their start and end apart: 19, of which 9 were waited for; matrix products, arithmetic and copies ran while one was open for 41% of the time, Pallas kernels for 0%

commit v1 on v0

v1 whole, which is shorter than its diff:
```python
import functools

import jax
import jax.numpy as jnp
from jax import lax
from jax.experimental import pallas as pl
from jax.experimental.pallas import tpu as pltpu
from jax.sharding import PartitionSpec as P

F32 = jnp.float32
BF16 = jnp.bfloat16
HD = 64
LANES = 128
BIG = 1e30
EPSILON = 1e-05
MIB = 1 << 20

ANY = pl.BlockSpec(memory_space=pl.ANY)
VMEM = pl.BlockSpec(memory_space=pltpu.VMEM)


def nn(left, right):
    return lax.dot_general(left, right, (((1,), (0,)), ((), ())), preferred_element_type=F32)


def nt(left, right):
    return lax.dot_general(left, right, (((1,), (1,)), ((), ())), preferred_element_type=F32)


def tn(left, right):
    return lax.dot_general(left, right, (((0,), (0,)), ((), ())), preferred_element_type=F32)


def unit_of(values):
    center = values - jnp.mean(values, axis=-1, keepdims=True)
    inverse = lax.rsqrt(jnp.mean(center * center, axis=-1, keepdims=True) + EPSILON)
    return center * inverse, inverse


def norm_back(scaled, unit, inverse):
    return inverse * (
        scaled
        - jnp.mean(scaled, axis=-1, keepdims=True)
        - unit * jnp.mean(scaled * unit, axis=-1, keepdims=True)
    )


def column_sum(values):
    return jnp.sum(values, axis=0, keepdims=True)


def needed(scal, block, rows):
    low, high = scal[0], scal[0] + scal[1] * rows
    return (block * rows < high) & ((block + 1) * rows > low)


def cost(flops, moved, transcendentals=0):
    return pl.CostEstimate(flops=int(flops), bytes_accessed=int(moved), transcendentals=int(transcendentals))


def qkv_kernel(seq, scal, x0, xl, xr, xll, xrr, weights, vec, q_out, k_out, v_out, buf, sems):
    i = pl.program_id(0)
    place = scal[2]
    rows, width = buf.shape[1:]
    share = width // weights.shape[0]

    def each(block, slot, act):
        for delta, ref in ((0, x0.at[seq]), (-1, xl), (1, xr), (-2, xll), (2, xrr)):

            @pl.when(needed(scal, block, rows) & (block - place == delta))
            def _():
                act(pltpu.make_async_copy(ref, buf.at[slot], sems.at[slot]))

    @pl.when(i == 0)
    def _():
        each(i, 0, lambda copy: copy.start())

    @pl.when(i + 1 < pl.num_programs(0))
    def _():
        each(i + 1, (i + 1) % 2, lambda copy: copy.start())

    each(i, i % 2, lambda copy: copy.wait())

    @pl.when(needed(scal, i, rows))
    def _():
        unit, _ = unit_of(buf[i % 2].astype(F32))
        act = (unit * vec[0:1] + vec[1:2]).astype(BF16)
        for j, out in enumerate((q_out, k_out, v_out)):
            weight = weights[:, j * share : (j + 1) * share, :].reshape(width, width)
            result = nn(act, weight)
            if j == 0:
                result = (result + vec[2:3]).astype(BF16) * jnp.asarray(HD**-0.5, BF16)
            if j == 2:
                result = result + vec[3:4]
            out[...] = result.astype(BF16)


def qkv_call(seq, scal, x, others, weights, vec):
    _, rows, width = x.shape
    blocks = 4
    out = jax.ShapeDtypeStruct((blocks * rows, width), BF16)
    spec = pl.BlockSpec((rows, width), lambda i, s: (i, 0))
    return pl.pallas_call(
        functools.partial(qkv_kernel, seq),
        out_shape=(out, out, out),
        grid_spec=pltpu.PrefetchScalarGridSpec(
            num_scalar_prefetch=1,
            grid=(blocks,),
            in_specs=[ANY] * 5
            + [
                pl.BlockSpec(weights.shape, lambda i, s: (0, 0, 0), pipeline_mode=pl.Buffered(1)),
                pl.BlockSpec(vec.shape, lambda i, s: (0, 0), pipeline_mode=pl.Buffered(1)),
            ],
            out_specs=[spec] * 3,
            scratch_shapes=[pltpu.VMEM((2, rows, width), BF16), pltpu.SemaphoreType.DMA((2,))],
        ),
        compiler_params=pltpu.CompilerParams(
            dimension_semantics=("arbitrary",), vmem_limit_bytes=24 * MIB
        ),
        cost_estimate=cost(6 * blocks * rows * width * width, 12e6),
        name="qkv",
    )(scal, x, *others, weights, vec)


def lane_is(*wanted):
    lane = lax.broadcasted_iota(jnp.int32, (1, LANES), 1)
    hit = lane == wanted[0]
    for other in wanted[1:]:
        hit = hit | (lane == other)
    return hit


def head_mask(which):
    lane = lax.broadcasted_iota(jnp.int32, (1, LANES), 1)
    return (lane < HD) if which == 0 else (lane >= HD)


def half(pair, which):
    return jnp.where(head_mask(which), pair, jnp.zeros_like(pair))


def window(scal, chunks, rows):
    return pl.ds(pl.multiple_of(scal[0], LANES), chunks * rows)


def by_chunks(scal, body):
    for chunks in range(1, 5):

        @pl.when(scal[1] == chunks)
        def _():
            body(chunks)


def attend_kernel(scal, q, k, v, seg, qf, o_out, qf_out, feats):
    pair = pl.program_id(0)
    rows = q.shape[0]

    @pl.when(pair == 0)
    def _():
        feats[...] = qf[...].astype(F32)

    def body(chunks):
        keys = window(scal, chunks, rows)
        k_aug = jnp.concatenate([k[keys, :], seg[keys, :]], axis=1)
        v_aug = jnp.concatenate([v[keys, :], jnp.ones((chunks * rows, LANES), BF16)], axis=1)
        parts = []
        for which in range(2):
            q_aug = jnp.concatenate([half(q[...], which), qf[...]], axis=1)
            scores = nt(q_aug, k_aug)
            highest = jnp.max(scores, axis=-1, keepdims=True)
            expon = jnp.exp(scores - highest).astype(BF16)
            both = nn(expon, v_aug)
            totals = both[:, LANES:]
            parts.append(both[:, :LANES] / totals)
            lse = highest + jnp.log(totals)
            top = lse.astype(BF16).astype(F32)
            lane = 16 + 4 * (2 * pair + which)
            feats[...] = jnp.where(
                lane_is(lane), -top, jnp.where(lane_is(lane + 1), top - lse, feats[...])
            )
        o_out[...] = jnp.where(head_mask(0), parts[0], parts[1]).astype(BF16)

    by_chunks(scal, body)

    @pl.when(pair == pl.num_programs(0) - 1)
    def _():
        qf_out[...] = feats[...].astype(BF16)


def attend_call(scal, q, k, v, seg, qf, rows):
    total, width = q.shape
    pairs = width // LANES
    own = pl.BlockSpec((rows, LANES), lambda p, s: (s[2], p))
    every = pl.BlockSpec((total, LANES), lambda p, s: (0, p))
    return pl.pallas_call(
        attend_kernel,
        out_shape=(
            jax.ShapeDtypeStruct((rows, width), BF16),
            jax.ShapeDtypeStruct((rows, LANES), BF16),
        ),
        grid_spec=pltpu.PrefetchScalarGridSpec(
            num_scalar_prefetch=1,
            grid=(pairs,),
            in_specs=[
                own,
                every,
                every,
                pl.BlockSpec((total, LANES), lambda p, s: (0, 0)),
                pl.BlockSpec((rows, LANES), lambda p, s: (0, 0)),
            ],
            out_specs=[
                pl.BlockSpec((rows, LANES), lambda p, s: (0, p)),
                pl.BlockSpec((rows, LANES), lambda p, s: (0, 0)),
            ],
            scratch_shapes=[pltpu.VMEM((rows, LANES), F32)],
        ),
        compiler_params=pltpu.CompilerParams(
            dimension_semantics=("arbitrary",), vmem_limit_bytes=24 * MIB
        ),
        cost_estimate=cost(16 * rows * total * width, 5e6, rows * total * width // HD),
        name="attend",
    )(scal, q, k, v, seg, qf)


def middle_kernel(
    seq, x, attn, grad, qf, weights, vec, out, msg, hid, gpre, act2, branch, gmid, sums,
    wo, up, down, hid_s, gpre_s, sems, out_sems,
):
    parts, share, width = wo.shape
    rows = attn.shape[0]
    loads = [pltpu.make_async_copy(weights.at[:, 0:share, :], wo, sems.at[0])]
    for c in range(4):
        loads.append(
            pltpu.make_async_copy(
                weights.at[:, (1 + c) * share : (2 + c) * share, :], up.at[c], sems.at[1 + c]
            )
        )
    loads.append(
        pltpu.make_async_copy(weights.at[:, 5 * share : 9 * share, :], down, sems.at[5])
    )
    for load in (loads[0], loads[1], loads[5], loads[2], loads[3], loads[4]):
        load.start()
    loads[0].wait()
    w_out = wo[...].reshape(width, width)
    middle = x[seq].astype(F32) + nn(attn[...], w_out) + vec[4:5]
    unit, inverse = unit_of(middle)
    normed = (unit * vec[5:6] + vec[6:7]).astype(BF16)
    act2[...] = normed
    g = grad[seq]
    g_full = g.astype(F32)
    result = middle + vec[7:8]
    grad_two = jnp.zeros((rows, width), F32)
    stores = []
    for c in range(4):
        loads[1 + c].wait()
        if c == 0:
            loads[5].wait()
        w_up = up[c].reshape(width, width)
        if parts >= 4:
            step = parts // 4
            w_down = down[c * step : (c + 1) * step].reshape(width, width)
        else:
            w_down = down[0, c * width : (c + 1) * width]
        pre = nn(normed, w_up) + vec[8 + c : 9 + c]
        whole = 0.5 * (1.0 + lax.erf(pre * 0.7071067811865476))
        slope = whole + pre * jnp.exp(-0.5 * pre * pre) * 0.3989422804014327
        hidden = (pre * whole).astype(BF16)
        hid_s[c] = hidden
        result = result + nn(hidden, w_down)
        grad_pre = (nt(g, w_down) * slope).astype(BF16)
        gpre_s[c] = grad_pre
        grad_two = grad_two + nt(grad_pre, w_up)
        sums[4 + c : 5 + c] = column_sum(grad_pre.astype(F32))
        stores.append(pltpu.make_async_copy(hid_s.at[c], hid.at[c], out_sems.at[0, c]))
        stores.append(pltpu.make_async_copy(gpre_s.at[c], gpre.at[c], out_sems.at[1, c]))
        stores[-1].start()
        stores[-2].start()
    out[...] = result.astype(BF16)
    sums[0:1] = column_sum(grad_two * unit)
    sums[1:2] = column_sum(grad_two)
    grad_middle = g_full + norm_back(grad_two * vec[5:6], unit, inverse)
    gmid[...] = grad_middle
    grad_branch = grad_middle.astype(BF16)
    branch[...] = grad_branch
    sums[2:3] = column_sum(grad_branch.astype(F32))
    sums[3:4] = column_sum(g_full)
    sums[8:16] = jnp.zeros((8, width), F32)
    grad_attn = nt(grad_branch, w_out).astype(BF16)
    msg[:, :width] = grad_attn
    product = grad_attn.astype(F32) * attn[...].astype(F32)
    high = product.astype(BF16)
    low = (product - high.astype(F32)).astype(BF16)
    head = lax.broadcasted_iota(jnp.int32, (width, LANES), 0) // HD
    lane = lax.broadcasted_iota(jnp.int32, (width, LANES), 1) - 16 - 4 * head
    pick = jnp.where((lane == 2) | (lane == 3), 1.0, 0.0).astype(BF16)
    delta = nn(high, pick) + nn(low, pick)
    top = delta.astype(BF16).astype(F32)
    column = lax.broadcasted_iota(jnp.int32, (1, LANES), 1)
    heads = width // HD
    in_heads = (column >= 16) & (column < 16 + 4 * heads)
    features = jnp.where(
        in_heads & (column % 4 == 2),
        -top,
        jnp.where(in_heads & (column % 4 == 3), top - delta, qf[...].astype(F32)),
    )
    msg[:, width:] = features.astype(BF16)
    for store in stores:
        store.wait()


def middle_call(seq, x, attn, grad, qf, weights, vec):
    _, rows, width = x.shape
    parts = weights.shape[0]
    share = width // parts
    flat = jax.ShapeDtypeStruct((rows, width), BF16)
    chunked = jax.ShapeDtypeStruct((4, rows, width), BF16)
    return pl.pallas_call(
        functools.partial(middle_kernel, seq),
        out_shape=(
            flat,
            jax.ShapeDtypeStruct((rows, width + LANES), BF16),
            chunked,
            chunked,
            flat,
            flat,
            jax.ShapeDtypeStruct((rows, width), F32),
            jax.ShapeDtypeStruct((16, width), F32),
        ),
        in_specs=[VMEM, VMEM, VMEM, VMEM, ANY, VMEM],
        out_specs=[VMEM, VMEM, ANY, ANY, VMEM, VMEM, VMEM, VMEM],
        scratch_shapes=[
            pltpu.VMEM((parts, share, width), BF16),
            pltpu.VMEM((4, parts, share, width), BF16),
            pltpu.VMEM((parts, 4 * share, width), BF16),
            pltpu.VMEM((4, rows, width), BF16),
            pltpu.VMEM((4, rows, width), BF16),
            pltpu.SemaphoreType.DMA((6,)),
            pltpu.SemaphoreType.DMA((2, 4)),
        ],
        compiler_params=pltpu.CompilerParams(vmem_limit_bytes=48 * MIB),
        cost_estimate=cost(2 * 18 * rows * width * width, 20e6, 2 * rows * 4 * width),
        name="middle",
    )(x, attn, grad, qf, weights, vec)


def ffn_grads_kernel(count, *refs):
    hid, gpre, act2, attn, branch = (refs[count * k : count * (k + 1)] for k in range(5))
    grad, first, second = refs[5 * count :]
    i = pl.program_id(0)

    @pl.when(i == 0)
    def _():
        total = sum(tn(attn[s][...], branch[s][...]) for s in range(count))
        first[...] = total.astype(BF16).reshape(first.shape)

    @pl.when(i > 0)
    def _():
        total = sum(tn(act2[s][...], gpre[s][0]) for s in range(count))
        first[...] = total.astype(BF16).reshape(first.shape)
        total = sum(tn(hid[s][0], grad[s]) for s in range(count))
        second[...] = total.astype(BF16).reshape(second.shape)


def ffn_grads_call(parts, hid, gpre, act2, attn, branch, grad):
    count, rows, width = grad.shape
    share = width // parts
    chunk = pl.BlockSpec((1, rows, width), lambda i: (jnp.maximum(i - 1, 0), 0, 0))
    whole = pl.BlockSpec((rows, width), lambda i: (0, 0))
    step = parts // 4 if parts >= 4 else 1
    depth = 4 * share if parts >= 4 else width
    second_map = (
        (lambda i: (jnp.maximum(i - 1, 0), 0, 0))
        if parts >= 4
        else (lambda i: (0, jnp.maximum(i - 1, 0), 0))
    )
    return pl.pallas_call(
        functools.partial(ffn_grads_kernel, count),
        out_shape=(
            jax.ShapeDtypeStruct((parts, 5 * share, width), BF16),
            jax.ShapeDtypeStruct((parts, 4 * share, width), BF16),
        ),
        grid=(5,),
        in_specs=[chunk] * (2 * count)
        + [whole] * (3 * count)
        + [pl.BlockSpec(grad.shape, lambda i: (0, 0, 0))],
        out_specs=[
            pl.BlockSpec((parts, share, width), lambda i: (0, i, 0)),
            pl.BlockSpec((step, depth, width), second_map),
        ],
        compiler_params=pltpu.CompilerParams(
            dimension_semantics=("arbitrary",), vmem_limit_bytes=40 * MIB
        ),
        cost_estimate=cost(18 * count * rows * width * width, 25e6),
        name="ffn_grads",
    )(*hid, *gpre, *act2, *attn, *branch, grad)


def ones_at(rows, *wanted):
    return jnp.broadcast_to(jnp.where(lane_is(*wanted), 1.0, 0.0).astype(BF16), (rows, LANES))


def query_grads_kernel(scal, q, k, v, grad, qf, seg, dq_out):
    pair = pl.program_id(0)
    rows = q.shape[0]

    def body(chunks):
        keys = window(scal, chunks, rows)
        size = chunks * rows
        k_pair, v_pair, features = k[keys, :], v[keys, :], seg[keys, :]
        total = None
        for which in range(2):
            lane = 16 + 4 * (2 * pair + which)
            q_aug = jnp.concatenate([half(q[...], which), qf[...]], axis=1)
            k_aug = jnp.concatenate([k_pair, features + ones_at(size, lane, lane + 1)], axis=1)
            probs = jnp.exp(nt(q_aug, k_aug))
            g_aug = jnp.concatenate([half(grad[...], which), qf[...]], axis=1)
            v_aug = jnp.concatenate([v_pair, ones_at(size, lane + 2, lane + 3)], axis=1)
            grad_scores = (probs * nt(g_aug, v_aug)).astype(BF16)
            part = nn(grad_scores, half(k_pair, which))
            total = part if total is None else total + part
        dq_out[...] = (total * HD**-0.5).astype(BF16)

    by_chunks(scal, body)


def query_grads_call(scal, q, k, v, msg, seg):
    total, width = q.shape
    rows = msg.shape[0]
    pairs = width // LANES
    every = pl.BlockSpec((total, LANES), lambda p, s: (0, p))
    return pl.pallas_call(
        query_grads_kernel,
        out_shape=jax.ShapeDtypeStruct((rows, width), BF16),
        grid_spec=pltpu.PrefetchScalarGridSpec(
            num_scalar_prefetch=1,
            grid=(pairs,),
            in_specs=[
                pl.BlockSpec((rows, LANES), lambda p, s: (s[2], p)),
                every,
                every,
                pl.BlockSpec((rows, LANES), lambda p, s: (0, p)),
                pl.BlockSpec((rows, LANES), lambda p, s: (0, pairs)),
                pl.BlockSpec((total, LANES), lambda p, s: (0, 0)),
            ],
            out_specs=pl.BlockSpec((rows, LANES), lambda p, s: (0, p)),
        ),
        compiler_params=pltpu.CompilerParams(
            dimension_semantics=("arbitrary",), vmem_limit_bytes=24 * MIB
        ),
        cost_estimate=cost(24 * rows * total * width, 5e6, rows * total * width // HD),
        name="query_grads",
    )(scal, q, k, v, msg, msg, seg)


def key_grads_kernel(scal, q, k, v, seg, g0, gl, gr, gll, grr, dk_out, dv_out, grads, sems):
    pair = pl.program_id(0)
    rows = k.shape[0]
    width = grads.shape[1] - LANES

    @pl.when(pair == 0)
    def _():
        for act in (lambda copy: copy.start(), lambda copy: copy.wait()):
            for block in range(4):
                for delta, ref in ((0, g0), (-1, gl), (1, gr), (-2, gll), (2, grr)):

                    @pl.when(needed(scal, block, rows) & (block - scal[2] == delta))
                    def _():
                        target = grads.at[pl.ds(block * rows, rows)]
                        act(pltpu.make_async_copy(ref, target, sems.at[block]))

    def body(chunks):
        queries = window(scal, chunks, rows)
        q_pair = q[queries, :]
        g_pair = grads[queries, pl.ds(pl.multiple_of(pair * LANES, LANES), LANES)]
        features = grads[queries, width:]
        dk, dv = None, None
        for which in range(2):
            lane = 16 + 4 * (2 * pair + which)
            q_half, g_half = half(q_pair, which), half(g_pair, which)
            k_aug = jnp.concatenate([k[...], seg[...] + ones_at(rows, lane, lane + 1)], axis=1)
            v_aug = jnp.concatenate([v[...], ones_at(rows, lane + 2, lane + 3)], axis=1)
            probs = jnp.exp(nt(k_aug, jnp.concatenate([q_half, features], axis=1)))
            grad_probs = nt(v_aug, jnp.concatenate([g_half, features], axis=1))
            grad_scores = (probs * grad_probs).astype(BF16)
            dv_part, dk_part = nn(probs.astype(BF16), g_half), nn(grad_scores, q_half)
            dk = dk_part if dk is None else dk + dk_part
            dv = dv_part if dv is None else dv + dv_part
        dk_out[...] = dk.astype(BF16)
        dv_out[...] = dv.astype(BF16)

    by_chunks(scal, body)


def key_grads_call(scal, q, k, v, seg, msgs):
    total, width = q.shape
    rows = msgs[0].shape[0]
    pairs = width // LANES
    own = pl.BlockSpec((rows, LANES), lambda p, s: (s[2], p))
    out = pl.BlockSpec((rows, LANES), lambda p, s: (0, p))
    return pl.pallas_call(
        key_grads_kernel,
        out_shape=(jax.ShapeDtypeStruct((rows, width), BF16),) * 2,
        grid_spec=pltpu.PrefetchScalarGridSpec(
            num_scalar_prefetch=1,
            grid=(pairs,),
            in_specs=[
                pl.BlockSpec((total, LANES), lambda p, s: (0, p)),
                own,
                own,
                pl.BlockSpec((rows, LANES), lambda p, s: (s[2], 0)),
            ]
            + [ANY] * 5,
            out_specs=[out, out],
            scratch_shapes=[
                pltpu.VMEM((total, width + LANES), BF16),
                pltpu.SemaphoreType.DMA((4,)),
            ],
        ),
        compiler_params=pltpu.CompilerParams(
            dimension_semantics=("arbitrary",), vmem_limit_bytes=28 * MIB
        ),
        cost_estimate=cost(32 * rows * total * width, 6e6, rows * total * width // HD),
        name="key_grads",
    )(scal, q, k, v, seg, *msgs)


def last_kernel(count, x, gmid, dq, dk, dv, weights, vec, sums, gin, grads, acc_q, acc_k, acc_v, acc_s):
    i = pl.program_id(0)
    parts, _, width = weights.shape
    share = width // parts
    unit, inverse = unit_of(x[0].astype(F32))
    act = (unit * vec[0:1] + vec[1:2]).astype(BF16)
    given = [dq[0], dk[0], dv[0]]
    accs = (acc_q, acc_k, acc_v)
    grad_one = jnp.zeros(unit.shape, F32)
    for j in range(3):
        weight = weights[:, j * share : (j + 1) * share, :].reshape(width, width)
        grad_one = grad_one + nt(given[j], weight)
        part = tn(act, given[j])

        @pl.when(i == 0)
        def _():
            accs[j][...] = part

        @pl.when(i > 0)
        def _():
            accs[j][...] += part

    gin[0] = (gmid[0] + norm_back(grad_one * vec[0:1], unit, inverse)).astype(BF16)
    rows_now = [
        column_sum(grad_one * unit),
        column_sum(grad_one),
        column_sum(given[0].astype(F32)),
        column_sum(given[2].astype(F32)),
    ]

    @pl.when(i == 0)
    def _():
        acc_s[...] = jnp.zeros(acc_s.shape, F32)

    acc_s[0:8] += sums[0, 0:8]
    for j, row in enumerate(rows_now):
        acc_s[8 + j : 9 + j] += row

    @pl.when(i == count - 1)
    def _():
        for j in range(3):
            grads[:, j * share : (j + 1) * share, :] = (
                accs[j][...].astype(BF16).reshape(parts, share, width)
            )
        total = acc_s[...].astype(BF16)
        for part in range(parts):
            grads[part, 3 * share : 3 * share + 16, :] = total


def last_call(x, gmid, dq, dk, dv, weights, vec, sums):
    count, rows, width = x.shape
    parts, depth, _ = weights.shape
    block = pl.BlockSpec((1, rows, width), lambda i: (i, 0, 0))
    fixed3 = lambda i: (0, 0, 0)
    return pl.pallas_call(
        functools.partial(last_kernel, count),
        out_shape=(
            jax.ShapeDtypeStruct(x.shape, BF16),
            jax.ShapeDtypeStruct((parts, depth, width), BF16),
        ),
        grid=(count,),
        in_specs=[
            block,
            block,
            block,
            block,
            block,
            pl.BlockSpec(weights.shape, fixed3, pipeline_mode=pl.Buffered(1)),
            pl.BlockSpec(vec.shape, lambda i: (0, 0)),
            pl.BlockSpec((1, 16, width), lambda i: (i, 0, 0)),
        ],
        out_specs=[block, pl.BlockSpec((parts, depth, width), fixed3)],
        scratch_shapes=[pltpu.VMEM((width, width), F32)] * 3 + [pltpu.VMEM((16, width), F32)],
        compiler_params=pltpu.CompilerParams(
            dimension_semantics=("arbitrary",), vmem_limit_bytes=48 * MIB
        ),
        cost_estimate=cost(12 * count * rows * width * width, 20e6),
        name="last",
    )(x, gmid, dq, dk, dv, weights, vec, sums)


def shifted(array, pairs):
    return lax.ppermute(array, "seq", pairs)


RIGHT = [(0, 1), (1, 2), (2, 3)]
LEFT = [(1, 0), (2, 1), (3, 2)]
RIGHT_AGAIN = [(1, 2), (2, 3)]
LEFT_AGAIN = [(2, 1), (1, 0)]


def neighbours(array):
    left, right = shifted(array, RIGHT), shifted(array, LEFT)
    return left, right, shifted(left, RIGHT_AGAIN), shifted(right, LEFT_AGAIN)


def whole_segments(segments, place):
    seqs, rows = segments.shape
    left, right = shifted(segments, RIGHT), shifted(segments, LEFT)
    far = shifted(segments, [(0, 2), (1, 3), (2, 0), (3, 1)])
    blocks = []
    for i in range(4):
        delta = i - place
        value = jnp.where(delta == 0, segments, jnp.where(delta == -1, left, right))
        value = jnp.where(jnp.abs(delta) == 2, far, value)
        value = jnp.where(delta == -3, -1, jnp.where(delta == 3, 99, value))
        blocks.append(value)
    return jnp.stack(blocks, axis=1).reshape(seqs, 4 * rows)


def windows(whole, segments, place, me, rows):
    first, last = segments[:, :1], segments[:, -1:]
    low = jnp.sum((whole < first).astype(jnp.int32), axis=1)
    high = jnp.sum((whole <= last).astype(jnp.int32), axis=1)
    start = (low // LANES) * LANES
    chunks = (high - start + rows - 1) // rows
    end = jnp.where(place == 0, 3 * rows, 4 * rows)
    start = jnp.minimum(start, end - chunks * rows)
    other = jnp.zeros_like(start)
    return jnp.stack([start, chunks, other + place, other + me], axis=1)


def per_device(
    inputs,
    segment_ids,
    norm1_gain,
    norm1_shift,
    query_weight,
    query_bias,
    key_weight,
    value_weight,
    value_bias,
    out_weight,
    out_bias,
    norm2_gain,
    norm2_shift,
    fc1_weight,
    fc1_bias,
    fc2_weight,
    fc2_bias,
    grad_output,
):
    seqs, rows, width = inputs.shape
    devices = lax.axis_size("dp")
    share = query_weight.shape[0]
    place, me = lax.axis_index("seq"), lax.axis_index("dp")
    direct = share % 16 == 0

    small = jnp.concatenate(
        [
            norm1_gain, norm1_shift, query_bias, value_bias,
            out_bias, norm2_gain, norm2_shift, fc2_bias, fc1_bias,
        ]
    )
    small = jnp.pad(small, (0, 16 * width - small.shape[0])).reshape(16, width)
    first_part = jnp.concatenate([query_weight, key_weight, value_weight, small])
    up_part = fc1_weight.reshape(share, 4, width).transpose(1, 0, 2).reshape(4 * share, width)
    second_part = jnp.concatenate([out_weight, up_part, fc2_weight])
    others = [neighbours(inputs[s]) for s in range(seqs)]
    whole = whole_segments(segment_ids, place)

    first = lax.all_gather(first_part, "dp", axis=0)
    second = lax.all_gather(second_part, "dp", axis=0)

    small_all = first[:, 3 * share :, :].reshape(devices, -1)
    eight = small_all[:, : 8 * share].reshape(devices, 8, share).transpose(1, 0, 2).reshape(8, width)
    four = small_all[:, 8 * share : 12 * share].reshape(4, width)
    vec = jnp.concatenate([eight, four, four]).astype(F32)
    if not direct:
        first = jnp.concatenate(
            [first[:, j * share : (j + 1) * share].reshape(width, width) for j in range(3)]
            + [jnp.zeros((16, width), BF16)]
        )[None]
        second = jnp.concatenate(
            [second[:, j * share : (j + 1) * share].reshape(width, width) for j in range(5)]
            + [second[:, 5 * share :].reshape(4 * width, width)]
        )[None]
    parts = first.shape[0]

    scal = windows(whole, segment_ids, place, me, rows)
    lane = lax.broadcasted_iota(jnp.int32, (1, 1, LANES), 2)
    seg = (whole[:, :, None] == lane).astype(BF16)
    qf = jnp.where((lane < 4) & (lane != segment_ids[:, :, None]), -BIG, 0.0).astype(BF16)

    saved, outs = [], []
    for s in range(seqs):
        q, k, v = qkv_call(s, scal[s], inputs, others[s], first, vec)
        attn, qf_s = attend_call(scal[s], q, k, v, seg[s], qf[s], rows)
        saved.append((q, k, v, attn))
        outs.append(middle_call(s, inputs, attn, grad_output, qf_s, second, vec))
    out, msg, hid, gpre, act2, branch, gmid, sums = zip(*outs)
    grads = [neighbours(msg[s]) for s in range(seqs)]
    attn = [saved[s][3] for s in range(seqs)]
    ffn_one, ffn_two = ffn_grads_call(parts, hid, gpre, act2, attn, branch, grad_output)
    dq = [query_grads_call(scal[s], *saved[s][:3], msg[s], seg[s]) for s in range(seqs)]
    dkv = [
        key_grads_call(scal[s], *saved[s][:3], seg[s], (msg[s], *grads[s])) for s in range(seqs)
    ]
    grad_inputs, proj = last_call(
        inputs,
        jnp.stack(gmid),
        jnp.stack(dq),
        jnp.stack([pair[0] for pair in dkv]),
        jnp.stack([pair[1] for pair in dkv]),
        first,
        vec,
        jnp.stack(sums),
    )
    if direct:
        ffn_all = jnp.concatenate([ffn_one, ffn_two], axis=1)
    else:
        ffn_all = jnp.concatenate(
            [ffn_one[0].reshape(5, devices, share, width).transpose(1, 0, 2, 3).reshape(devices, 5 * share, width),
             ffn_two[0].reshape(devices, 4 * share, width)], axis=1)
        total = proj[0, 3 * width :]
        proj = jnp.concatenate(
            [proj[0, : 3 * width].reshape(3, devices, share, width).transpose(1, 0, 2, 3).reshape(devices, 3 * share, width),
             jnp.broadcast_to(total[None], (devices, 16, width))], axis=1)

    def reduced(array):
        part = lax.psum_scatter(array, "dp", scatter_dimension=0, tiled=True)[0]
        return lax.psum(part, "seq").astype(F32)

    ffn_done = reduced(ffn_all)
    proj_done = reduced(proj)
    vectors = proj_done[3 * share :]
    mine = lax.dynamic_slice(vectors, (0, me * share), (16, share))
    up_grad = ffn_done[share : 5 * share].reshape(4, share, width).transpose(1, 0, 2)
    up_bias = lax.dynamic_slice(vectors[4:8].reshape(4 * width), (me * 4 * share,), (4 * share,))
    return (
        jnp.stack(out),
        grad_inputs,
        mine[8],
        mine[9],
        proj_done[:share],
        mine[10],
        proj_done[share : 2 * share],
        proj_done[2 * share : 3 * share],
        mine[11],
        ffn_done[:share],
        mine[2],
        mine[0],
        mine[1],
        up_grad.reshape(share, 4 * width),
        up_bias,
        ffn_done[5 * share :],
        mine[3],
    )


def solution(mesh):
    token, matrix, vector = P("dp", "seq", None), P("dp", None), P("dp")
    return jax.shard_map(
        per_device,
        mesh=mesh,
        in_specs=(
            token, P("dp", "seq"), vector, vector, matrix, vector, matrix, matrix, vector,
            matrix, vector, vector, vector, matrix, vector, matrix, vector, token,
        ),
        out_specs=(
            token, token, vector, vector, matrix, vector, matrix, matrix, vector,
            matrix, vector, vector, vector, matrix, vector, matrix, vector,
        ),
        check_vma=False,
    )
```

time: 1110 us -> 504 us (0.45)
  matrix products: 266 us -> 0 us
  blocking collectives: 219 us -> 0 us
  Pallas kernels: 0 us -> 129 us
  local copies, waits for them, and re-layouts: 172 us -> 46.4 us
  waiting for transfers between devices: 323 us -> 222 us
  other arithmetic: 68 us -> 16.8 us
  starting transfers between devices: 27.8 us -> 67.2 us
    dot_general x81 -> x0, matrix products: 266 us -> none  [the longest x18 38.3 us: masked_scores(): jnp.einsum('qd,kd->qk', query_pair, key_pair, preferred_element_type=jnp....]
    all_to_all x6 -> x0, waiting for transfers between devices: 156 us -> none  [the longest x1 45.5 us: per_device(): lax.all_to_all(from_pairs(grad_query_pairs, seqs_here, heads_here), 'seq'...]
    pallas_call x0 -> x17, Pallas kernels: none -> 129 us  [the longest x3 31.3 us: middle_call(): pl.pallas_call(functools.partial(middle_kernel, seq), out_shape=(flat, ja...]
    all_to_all x2 -> x0, blocking collectives: 102 us -> none  [the longest x1 51.5 us: per_device(): lax.all_to_all(from_pairs(grad_key_pairs, seqs_here, heads_here), 'seq',...]
    psum x1, waiting for transfers between devices: 8.2 us -> 78.2 us  [reduced(): return lax.psum(part, 'seq').astype(F32)]
    ppermute x0 -> x27, starting transfers between devices: none -> 67 us  [shifted(): return lax.ppermute(array, 'seq', pairs)]
    reshape x17 -> x8, local copies, waits for them, and re-layouts: 56.3 us -> 1.43 us  [the longest x1 1.13 us: per_device(): up_grad.reshape(share, 4 * width)]
    unnamed x2 -> x0, blocking collectives: 52.5 us -> none
  transfers between devices with their start and end apart: 19 -> 32, of which waited for: 9 -> 11; matrix products, arithmetic and copies ran while one was open for 41% -> 3% of each run, Pallas kernels for 0% -> 18%
where the time goes in v1:
time: 504 us; the launch traced here: 497 us
  waiting for transfers between devices  222 us (44%)
  Pallas kernels  129 us (26%)
  starting transfers between devices  67.2 us (13%)
  local copies, waits for them, and re-layouts  46.4 us (9%)
  other arithmetic  16.8 us (3%)
  between operations  15.1 us (3%)
    reduce_scatter x2, waiting for transfers between devices, reduced(): part = lax.psum_scatter(array, 'dp', scatter_dimension=0, tiled=True)[0]  113 us
    psum x1, waiting for transfers between devices, reduced(): return lax.psum(part, 'seq').astype(F32)  78.2 us
    ppermute x27, starting transfers between devices, shifted(): return lax.ppermute(array, 'seq', pairs)  67 us
    pallas_call x3, Pallas kernels, middle_call(): pl.pallas_call(functools.partial(middle_kernel, seq), out_shape=(flat, ja...  31.3 us
    unnamed x126, local copies, waits for them, and re-layouts  30.5 us
    ppermute x27, waiting for transfers between devices, shifted(): return lax.ppermute(array, 'seq', pairs)  24.2 us
    pallas_call x3, Pallas kernels, key_grads_call(): pl.pallas_call(key_grads_kernel, out_shape=(jax.ShapeDtypeStruct((rows, w...  21.5 us
    pallas_call x3, Pallas kernels, attend_call(): pl.pallas_call(attend_kernel, out_shape=(jax.ShapeDtypeStruct((rows, widt...  18.5 us
  transfers between devices with their start and end apart: 32, of which 11 were waited for; matrix products, arithmetic and copies ran while one was open for 3% of the time, Pallas kernels for 18%

profile of v1, /device:TPU:0, one launch (start us, length us, event | category | flops | bytes accessed | tf_op | source)
XLA Modules:
  0.0 496.8 jit_solution(6057084010007695728)
XLA Ops:
  7.3 6.2 %concatenate.15 = bf16[1152]{0:T(1024)(128)(2,1)S(1)} concatenate(bf16[96]{0:T(256)(128)(2,1)} %param.20, bf16[96]{0:T(256)(128)(2,1)} %param.21, bf16[96]{0:T(256)(128)(2,1)} %param.23, bf16[96]{0:T(256)(128)(2,1)} %param.26, bf16[96]{0:T(256)(128)(2,1)} %param.28, bf16[96]{0:T(256)(128)(2,1)} %param.29, bf16[96]{0:T(256)(128)(2,1)} %param.30, bf16[96]{0:T(256)(128)(2,1)} %param.34, ...), dimensions={0} | concatenate | bytes 4608 | tf_op jit(solution)/shard_map/concatenate | solution.py:675
  13.5 1.9 pad_maximum_fusion.7
  18.1 5.6 %collective-permute-start.1 = (s32[3,256]{1,0:T(4,128)S(1)}, s32[3,256]{1,0:T(4,128)S(1)}, u32[]{:S(2)}, u32[]{:S(2)}) collective-permute-start(s32[3,256]{1,0:T(4,128)S(1)} %copy-done.61), channel_id=1, source_target_pairs={{0,1},{1,2},{2,3},{4,5},{5,6},{6,7},{8,9},{9,10},{10,11},{12,13},{... | collective-permute-start | bytes 9224 | tf_op jit(solution)/shard_map/ppermute | solution.py:609
  23.7 3.1 collective-permute-start
  29.0 5.3 %collective-permute-start.11 = (bf16[256,768]{1,0:T(8,128)(2,1)}, bf16[256,768]{1,0:T(8,128)(2,1)}, u32[]{:S(2)}, u32[]{:S(2)}) collective-permute-start(bf16[256,768]{1,0:T(8,128)(2,1)} %get-tuple-element.128), channel_id=1, source_target_pairs={{0,1},{1,2},{2,3},{4,5},{5,6},{6,7},{8,9},{9,10},{10,11},{12,13},{... | collective-permute-start | bytes 1179656 | tf_op jit(solution)/shard_map/ppermute | solution.py:609
  36.2 4.6 collective-permute-start.7
  43.1 13.7 %collective-permute-done.4.xr = bf16[256,768]{1,0:T(8,128)(2,1)} collective-permute-done((bf16[256,768]{1,0:T(8,128)(2,1)}, bf16[256,768]{1,0:T(8,128)(2,1)}, u32[]{:S(2)}, u32[]{:S(2)}) %collective-permute-start.4) | collective-permute-done | bytes 393248 | tf_op jit(solution)/shard_map/ppermute | solution.py:609
  56.8 2.3 collective-permute-start.3
  60.4 1.4 collective-permute-start.9
  66.8 4.4 collective-permute-done.10.xrr
  72.5 2.0 copy-done.1
  76.6 3.9 qkv.4
  80.6 3.7 qkv.5
  84.4 6.1 %attend.4 = (bf16[256,768]{1,0:T(8,128)(2,1)S(1)}, bf16[256,128]{1,0:T(8,128)(2,1)S(1)}) custom-call(s32[4]{0:T(128)S(1)} %get-tuple-element.121.scal, bf16[1024,768]{1,0:T(8,128)(2,1)S(1)} %get-tuple-element.72.q, bf16[1024,768]{1,0:T(8,128)(2,1)S(1)} %get-tuple-element.73.k, bf16[1024,768]{1,0:T(8,128)(2,1)S(1)} %get-tuple-element.74.v, ...), custom_call_target="tpu_custom_call" | custom-call | flops 3221225472 | bytes 5000000 | tf_op jit(solution)/shard_map/attend/pallas_call | solution.py:195
  91.3 6.1 %attend.5 = (bf16[256,768]{1,0:T(8,128)(2,1)S(1)}, bf16[256,128]{1,0:T(8,128)(2,1)S(1)}) custom-call(s32[4]{0:T(128)S(1)} %get-tuple-element.120.scal, bf16[1024,768]{1,0:T(8,128)(2,1)S(1)} %get-tuple-element.78.q, bf16[1024,768]{1,0:T(8,128)(2,1)S(1)} %get-tuple-element.79.k, bf16[1024,768]{1,0:T(8,128)(2,1)S(1)} %get-tuple-element.80.v, ...), custom_call_target="tpu_custom_call" | custom-call | flops 3221225472 | bytes 5000000 | tf_op jit(solution)/shard_map/attend/pallas_call | solution.py:195
  98.2 3.7 qkv.3
  101.9 6.3 %attend.3 = (bf16[256,768]{1,0:T(8,128)(2,1)S(1)}, bf16[256,128]{1,0:T(8,128)(2,1)S(1)}) custom-call(s32[4]{0:T(128)S(1)} %get-tuple-element.119.scal, bf16[1024,768]{1,0:T(8,128)(2,1)S(1)} %get-tuple-element.66.q, bf16[1024,768]{1,0:T(8,128)(2,1)S(1)} %get-tuple-element.67.k, bf16[1024,768]{1,0:T(8,128)(2,1)S(1)} %get-tuple-element.68.v, ...), custom_call_target="tpu_custom_call" | custom-call | flops 3221225472 | bytes 5000000 | tf_op jit(solution)/shard_map/attend/pallas_call | solution.py:195
  111.7 7.1 %all-gather.7.cloned.1.call-done = bf16[6912,768]{1,0:T(8,128)(2,1)} async-done(((bf16[864,768]{1,0:T(8,128)(2,1)}), bf16[6912,768]{1,0:T(8,128)(2,1)}) %all-gather.7.cloned.1.call-update) | async-done | bytes 10616848 | tf_op jit(solution)/shard_map/all_gather | solution.py:689
  120.1 10.5 %middle.3 = (bf16[256,768]{1,0:T(8,128)(2,1)S(1)}, bf16[256,896]{1,0:T(8,128)(2,1)S(1)}, bf16[4,256,768]{2,1,0:T(8,128)(2,1)}, bf16[4,256,768]{2,1,0:T(8,128)(2,...) custom-call(bf16[3,256,768]{2,1,0:T(8,128)(2,1)S(1)} %copy-done, ...), custom_call_target="tpu_custom_call" | custom-call | flops 5435817984 | bytes 20000000 | tf_op jit(solution)/shard_map/middle/pallas_call | solution.py:317
  131.4 6.1 %query_grads.3 = bf16[256,768]{1,0:T(8,128)(2,1)S(1)} custom-call(s32[4]{0:T(128)S(1)} %get-tuple-element.119.scal, bf16[1024,768]{1,0:T(8,128)(2,1)S(1)} %copy-done.29, bf16[1024,768]{1,0:T(8,128)(2,1)S(1)} %copy-done.32, bf16[1024,768]{1,0:T(8,128)(2,1)S(1)} %copy-done.35, bf16[256,896]{1,0:T(8,128)(2,1)S(1)} %get-tuple-element.87.grad.qf.g0, ...), custom_call_target="tpu_custom_call" | custom-call | flops 4831838208 | bytes 5000000 | tf_op jit(solution)/shard_map/query_grads/pallas_call | solution.py:431
  138.8 12.2 %collective-permute-start.15 = (bf16[256,896]{1,0:T(8,128)(2,1)S(1)}, bf16[256,896]{1,0:T(8,128)(2,1)S(1)}, u32[]{:S(2)}, u32[]{:S(2)}) collective-permute-start(bf16[256,896]{1,0:T(8,128)(2,1)S(1)} %get-tuple-element.87.grad.qf.g0), channel_id=1, source_target_pairs={{0,1},{1,2},{2,3},{4,5},{5,6},{6,7},{8,9},{9,10},{10,11},{12,13},{... | collective-permute-start | bytes 1376264 | tf_op jit(solution)/shard_map/ppermute | solution.py:609
  151.0 10.4 %middle.5 = (bf16[256,768]{1,0:T(8,128)(2,1)S(1)}, bf16[256,896]{1,0:T(8,128)(2,1)S(1)}, bf16[4,256,768]{2,1,0:T(8,128)(2,1)}, bf16[4,256,768]{2,1,0:T(8,128)(2,...) custom-call(bf16[3,256,768]{2,1,0:T(8,128)(2,1)S(1)} %copy-done, ...), custom_call_target="tpu_custom_call" | custom-call | flops 5435817984 | bytes 20000000 | tf_op jit(solution)/shard_map/middle/pallas_call | solution.py:317
  162.7 5.0 %collective-permute-start.23 = (bf16[256,896]{1,0:T(8,128)(2,1)S(1)}, bf16[256,896]{1,0:T(8,128)(2,1)S(1)}, u32[]{:S(2)}, u32[]{:S(2)}) collective-permute-start(bf16[256,896]{1,0:T(8,128)(2,1)S(1)} %get-tuple-element.89.grad.qf.g0), channel_id=1, source_target_pairs={{0,1},{1,2},{2,3},{4,5},{5,6},{6,7},{8,9},{9,10},{10,11},{12,13},{... | collective-permute-start | bytes 1376264 | tf_op jit(solution)/shard_map/ppermute | solution.py:609
  167.7 10.4 %middle.4 = (bf16[256,768]{1,0:T(8,128)(2,1)S(1)}, bf16[256,896]{1,0:T(8,128)(2,1)S(1)}, bf16[4,256,768]{2,1,0:T(8,128)(2,1)}, bf16[4,256,768]{2,1,0:T(8,128)(2,...) custom-call(bf16[3,256,768]{2,1,0:T(8,128)(2,1)S(1)} %copy-done, ...), custom_call_target="tpu_custom_call" | custom-call | flops 5435817984 | bytes 20000000 | tf_op jit(solution)/shard_map/middle/pallas_call | solution.py:317
  180.2 1.5 pad_maximum_fusion.1.gmid
  183.4 5.9 %query_grads.5 = bf16[256,768]{1,0:T(8,128)(2,1)S(1)} custom-call(s32[4]{0:T(128)S(1)} %get-tuple-element.120.scal, bf16[1024,768]{1,0:T(8,128)(2,1)S(1)} %copy-done.23, bf16[1024,768]{1,0:T(8,128)(2,1)S(1)} %copy-done.25, bf16[1024,768]{1,0:T(8,128)(2,1)S(1)} %copy-done.27, bf16[256,896]{1,0:T(8,128)(2,1)S(1)} %get-tuple-element.89.grad.qf.g0, ...), custom_call_target="tpu_custom_call" | custom-call | flops 4831838208 | bytes 5000000 | tf_op jit(solution)/shard_map/query_grads/pallas_call | solution.py:431
  189.3 6.7 %collective-permute-start.19 = (bf16[256,896]{1,0:T(8,128)(2,1)S(1)}, bf16[256,896]{1,0:T(8,128)(2,1)S(1)}, u32[]{:S(2)}, u32[]{:S(2)}) collective-permute-start(bf16[256,896]{1,0:T(8,128)(2,1)S(1)} %get-tuple-element.88.grad.qf.g0), channel_id=1, source_target_pairs={{0,1},{1,2},{2,3},{4,5},{5,6},{6,7},{8,9},{9,10},{10,11},{12,13},{... | collective-permute-start | bytes 1376264 | tf_op jit(solution)/shard_map/ppermute | solution.py:609
  196.0 1.3 collective-permute-start.18
  198.3 5.9 %query_grads.4 = bf16[256,768]{1,0:T(8,128)(2,1)S(1)} custom-call(s32[4]{0:T(128)S(1)} %get-tuple-element.121.scal, bf16[1024,768]{1,0:T(8,128)(2,1)S(1)} %copy-done.17, bf16[1024,768]{1,0:T(8,128)(2,1)S(1)} %copy-done.19, bf16[1024,768]{1,0:T(8,128)(2,1)S(1)} %copy-done.21, bf16[256,896]{1,0:T(8,128)(2,1)S(1)} %get-tuple-element.88.grad.qf.g0, ...), custom_call_target="tpu_custom_call" | custom-call | flops 4831838208 | bytes 5000000 | tf_op jit(solution)/shard_map/query_grads/pallas_call | solution.py:431
  207.5 1.7 collective-permute-done.18.grr
  209.9 7.1 %key_grads.3 = (bf16[256,768]{1,0:T(8,128)(2,1)S(1)}, bf16[256,768]{1,0:T(8,128)(2,1)S(1)}) custom-call(s32[4]{0:T(128)S(1)} %get-tuple-element.119.scal, bf16[1024,768]{1,0:T(8,128)(2,1)S(1)} %copy-done.30, bf16[1024,768]{1,0:T(8,128)(2,1)S(1)} %copy-done.33, bf16[1024,768]{1,0:T(8,128)(2,1)S(1)} %copy-done.36, ...), custom_call_target="tpu_custom_call" | custom-call | flops 6442450944 | bytes 6000000 | tf_op jit(solution)/shard_map/key_grads/pallas_call | solution.py:500
  217.0 1.4 collective-permute-done.26.grr
  218.5 7.1 %key_grads.5 = (bf16[256,768]{1,0:T(8,128)(2,1)S(1)}, bf16[256,768]{1,0:T(8,128)(2,1)S(1)}) custom-call(s32[4]{0:T(128)S(1)} %get-tuple-element.120.scal, bf16[1024,768]{1,0:T(8,128)(2,1)S(1)} %copy-done.23, bf16[1024,768]{1,0:T(8,128)(2,1)S(1)} %copy-done.25, bf16[1024,768]{1,0:T(8,128)(2,1)S(1)} %copy-done.27, ...), custom_call_target="tpu_custom_call" | custom-call | flops 6442450944 | bytes 6000000 | tf_op jit(solution)/shard_map/key_grads/pallas_call | solution.py:500
  225.6 2.7 collective-permute-done.22.grr
  228.3 7.3 %key_grads.4 = (bf16[256,768]{1,0:T(8,128)(2,1)S(1)}, bf16[256,768]{1,0:T(8,128)(2,1)S(1)}) custom-call(s32[4]{0:T(128)S(1)} %get-tuple-element.121.scal, bf16[1024,768]{1,0:T(8,128)(2,1)S(1)} %copy-done.17, bf16[1024,768]{1,0:T(8,128)(2,1)S(1)} %copy-done.19, bf16[1024,768]{1,0:T(8,128)(2,1)S(1)} %copy-done.21, ...), custom_call_target="tpu_custom_call" | custom-call | flops 6442450944 | bytes 6000000 | tf_op jit(solution)/shard_map/key_grads/pallas_call | solution.py:500
  236.0 17.2 %last.1 = (bf16[3,256,768]{2,1,0:T(8,128)(2,1)}, bf16[8,304,768]{2,1,0:T(8,128)(2,1)}) custom-call(bf16[3,256,768]{2,1,0:T(8,128)(2,1)S(1)} %copy-done, f32[3,256,768]{2,1,0:T(8,128)} %pad_maximum_fusion.1.gmid, bf16[3,256,768]{2,1,0:T(8,128)(2,1)S(1)} %get-tuple-element.152.dq, bf16[3,256,768]{2,1,0:T(8,128)(2,1)S(1)} %get-tuple-element.153.dk, ...), custom_call_target="tpu_custom_call" | custom-call | flops 5435817984 | bytes 20000000 | tf_op jit(solution)/shard_map/last/pallas_call | solution.py:581
  254.9 1.4 copy-done.10
  256.3 1.4 copy-done.11
  257.7 1.4 copy-done.12
  259.1 1.4 copy-done.13
  260.5 1.4 copy-done.14
  261.9 1.4 copy-done.15
  269.3 11.3 %ffn_grads.1 = (bf16[8,480,768]{2,1,0:T(8,128)(2,1)}, bf16[8,384,768]{2,1,0:T(8,128)(2,1)}) custom-call(bf16[4,256,768]{2,1,0:T(8,128)(2,1)S(1)} %copy-done.10, bf16[4,256,768]{2,1,0:T(8,128)(2,1)S(1)} %copy-done.14, bf16[4,256,768]{2,1,0:T(8,128)(2,1)S(1)} %copy-done.12, bf16[4,256,768]{2,1,0:T(8,128)(2,1)S(1)} %copy-done.11, ...), custom_call_target="tpu_custom_call" | custom-call | flops 8153726976 | bytes 25000000 | tf_op jit(solution)/shard_map/ffn_grads/pallas_call | solution.py:376
  280.5 9.5 %pad_maximum_fusion = bf16[8,864,768]{2,1,0:T(8,128)(2,1)} fusion(bf16[8,384,768]{2,1,0:T(8,128)(2,1)} %get-tuple-element.114, bf16[8,480,768]{2,1,0:T(8,128)(2,1)} %get-tuple-element.113), kind=kLoop, calls=%fused_computation | loop fusion | flops 21233664 | bytes 21233664 | tf_op jit(solution)/shard_map/concatenate | solution.py:736
  290.1 26.6 %reduce-scatter.3.cloned.1.call-done = bf16[1,304,768]{2,1,0:T(8,128)(2,1)} async-done(((bf16[8,304,768]{2,1,0:T(8,128)(2,1)}), bf16[1,304,768]{2,1,0:T(8,128)(2,1)}) %reduce-scatter.3.cloned.1.call-update) | async-done | bytes 466960 | tf_op jit(solution)/shard_map/reduce_scatter | solution.py:747
  316.7 86.0 %reduce-scatter.5.cloned.1.call-done = bf16[1,864,768]{2,1,0:T(8,128)(2,1)} async-done(((bf16[8,864,768]{2,1,0:T(8,128)(2,1)}), bf16[1,864,768]{2,1,0:T(8,128)(2,1)}) %reduce-scatter.5.cloned.1.call-update) | async-done | bytes 1327120 | tf_op jit(solution)/shard_map/reduce_scatter | solution.py:747
  403.9 78.2 %all-reduce.4.cloned.1.call-done = (bf16[304,768]{1,0:T(8,128)(2,1)}, bf16[864,768]{1,0:T(8,128)(2,1)}) async-done(((bf16[304,768]{1,0:T(8,128)(2,1)}, bf16[864,768]{1,0:T(8,128)(2,1)}), (bf16[304,768]{1,0:T(8,128)(2,1)}, bf16[864,768]{1,0:T(8,128)(2,1)})) %all-reduce.4.cloned.1.call-update) | async-done | bytes 1794064 | tf_op jit(solution)/shard_map/psum | solution.py:748
  483.7 2.0 fusion.5
  (207 shorter events, 51.7 us)
Async XLA Ops:
  7.2 54.9 %all-gather.5.cloned.1.call-start = ((), (), s32[]{:S(2)}) async-start(), calls=%async_computation.4 | async-start | bytes 4202496 | tf_op jit(solution)/shard_map/all_gather | solution.py:688
  15.4 103.4 %all-gather.7.cloned.1.call-start = ((), (), s32[]{:S(2)}) async-start(), calls=%async_computation.5 | async-start | bytes 11943936 | tf_op jit(solution)/shard_map/all_gather | solution.py:689
  16.8 299.9 %reduce-scatter.3.cloned.1.call-start = ((), (), s32[]{:S(2)}) async-start(), calls=%async_computation.2 | async-start | bytes 4202496 | tf_op jit(solution)/shard_map/reduce_scatter | solution.py:747
  16.8 18.1 %collective-permute-start.2 = (s32[3,256]{1,0:T(4,128)S(1)}, s32[3,256]{1,0:T(4,128)S(1)}, u32[]{:S(2)}, u32[]{:S(2)}) collective-permute-start(s32[3,256]{1,0:T(4,128)S(1)} %copy-done.61), channel_id=1, source_target_pairs={{1,0},{2,1},{3,2},{5,4},{6,5},{7,6},{9,8},{10,9},{11,10},{13,12},{... | collective-permute-start | bytes 9224 | tf_op jit(solution)/shard_map/ppermute | solution.py:609
  18.1 18.1 %collective-permute-start.1 = (s32[3,256]{1,0:T(4,128)S(1)}, s32[3,256]{1,0:T(4,128)S(1)}, u32[]{:S(2)}, u32[]{:S(2)}) collective-permute-start(s32[3,256]{1,0:T(4,128)S(1)} %copy-done.61), channel_id=1, source_target_pairs={{0,1},{1,2},{2,3},{4,5},{5,6},{6,7},{8,9},{9,10},{10,11},{12,13},{... | collective-permute-start | bytes 9224 | tf_op jit(solution)/shard_map/ppermute | solution.py:609
  23.7 17.1 %collective-permute-start = (s32[3,256]{1,0:T(4,128)S(1)}, s32[3,256]{1,0:T(4,128)S(1)}, u32[]{:S(2)}, u32[]{:S(2)}) collective-permute-start(s32[3,256]{1,0:T(4,128)S(1)} %copy-done.61), channel_id=1, source_target_pairs={{0,2},{1,3},{2,0},{3,1},{4,6},{5,7},{6,4},{7,5},{8,10},{9,11},{10,... | collective-permute-start | bytes 9224 | tf_op jit(solution)/shard_map/ppermute | solution.py:609
  27.7 35.7 %collective-permute-start.12 = (bf16[256,768]{1,0:T(8,128)(2,1)}, bf16[256,768]{1,0:T(8,128)(2,1)}, u32[]{:S(2)}, u32[]{:S(2)}) collective-permute-start(bf16[256,768]{1,0:T(8,128)(2,1)} %get-tuple-element.128), channel_id=1, source_target_pairs={{1,0},{2,1},{3,2},{5,4},{6,5},{7,6},{9,8},{10,9},{11,10},{13,12},{... | collective-permute-start | bytes 1179656 | tf_op jit(solution)/shard_map/ppermute | solution.py:609
  29.0 35.7 %collective-permute-start.11 = (bf16[256,768]{1,0:T(8,128)(2,1)}, bf16[256,768]{1,0:T(8,128)(2,1)}, u32[]{:S(2)}, u32[]{:S(2)}) collective-permute-start(bf16[256,768]{1,0:T(8,128)(2,1)} %get-tuple-element.128), channel_id=1, source_target_pairs={{0,1},{1,2},{2,3},{4,5},{5,6},{6,7},{8,9},{9,10},{10,11},{12,13},{... | collective-permute-start | bytes 1179656 | tf_op jit(solution)/shard_map/ppermute | solution.py:609
  34.9 24.2 %collective-permute-start.8 = (bf16[256,768]{1,0:T(8,128)(2,1)S(1)}, bf16[256,768]{1,0:T(8,128)(2,1)S(1)}, u32[]{:S(2)}, u32[]{:S(2)}) collective-permute-start(bf16[256,768]{1,0:T(8,128)(2,1)S(1)} %get-tuple-element.129), channel_id=1, source_target_pairs={{1,0},{2,1},{3,2},{5,4},{6,5},{7,6},{9,8},{10,9},{11,10},{13,12},{... | collective-permute-start | bytes 1179656 | tf_op jit(solution)/shard_map/ppermute | solution.py:609
  36.2 24.2 %collective-permute-start.7 = (bf16[256,768]{1,0:T(8,128)(2,1)S(1)}, bf16[256,768]{1,0:T(8,128)(2,1)S(1)}, u32[]{:S(2)}, u32[]{:S(2)}) collective-permute-start(bf16[256,768]{1,0:T(8,128)(2,1)S(1)} %get-tuple-element.129), channel_id=1, source_target_pairs={{0,1},{1,2},{2,3},{4,5},{5,6},{6,7},{8,9},{9,10},{10,11},{12,13},{... | collective-permute-start | bytes 1179656 | tf_op jit(solution)/shard_map/ppermute | solution.py:609
  40.8 16.0 %collective-permute-start.4 = (bf16[256,768]{1,0:T(8,128)(2,1)}, bf16[256,768]{1,0:T(8,128)(2,1)}, u32[]{:S(2)}, u32[]{:S(2)}) collective-permute-start(bf16[256,768]{1,0:T(8,128)(2,1)} %get-tuple-element.127), channel_id=1, source_target_pairs={{1,0},{2,1},{3,2},{5,4},{6,5},{7,6},{9,8},{10,9},{11,10},{13,12},{... | collective-permute-start | bytes 1179656 | tf_op jit(solution)/shard_map/ppermute | solution.py:609
  56.8 8.8 %collective-permute-start.3 = (bf16[256,768]{1,0:T(8,128)(2,1)}, bf16[256,768]{1,0:T(8,128)(2,1)}, u32[]{:S(2)}, u32[]{:S(2)}) collective-permute-start(bf16[256,768]{1,0:T(8,128)(2,1)} %get-tuple-element.127), channel_id=1, source_target_pairs={{0,1},{1,2},{2,3},{4,5},{5,6},{6,7},{8,9},{9,10},{10,11},{12,13},{... | collective-permute-start | bytes 1179656 | tf_op jit(solution)/shard_map/ppermute | solution.py:609
  59.1 13.4 %copy-start.6 = (bf16[256,768]{1,0:T(8,128)(2,1)}, bf16[256,768]{1,0:T(8,128)(2,1)S(1)}, u32[]{:S(2)}) copy-start(bf16[256,768]{1,0:T(8,128)(2,1)S(1)} %collective-permute-done.8.xr) | copy-start | bytes 1179652
  59.1 12.1 %collective-permute-start.10 = (bf16[256,768]{1,0:T(8,128)(2,1)S(1)}, bf16[256,768]{1,0:T(8,128)(2,1)}, u32[]{:S(2)}, u32[]{:S(2)}) collective-permute-start(bf16[256,768]{1,0:T(8,128)(2,1)S(1)} %collective-permute-done.8.xr), channel_id=1, source_target_pairs={{2,1},{1,0},{6,5},{5,4},{10,9},{9,8},{14,13},{13,12},{18,17},{17,1... | collective-permute-start | bytes 1179656 | tf_op jit(solution)/shard_map/ppermute | solution.py:609
  60.4 12.1 %copy-start.8 = (bf16[256,768]{1,0:T(8,128)(2,1)}, bf16[256,768]{1,0:T(8,128)(2,1)S(1)}, u32[]{:S(2)}) copy-start(bf16[256,768]{1,0:T(8,128)(2,1)S(1)} %collective-permute-done.7.xl) | copy-start | bytes 1179652
  60.4 12.0 %collective-permute-start.9 = (bf16[256,768]{1,0:T(8,128)(2,1)S(1)}, bf16[256,768]{1,0:T(8,128)(2,1)}, u32[]{:S(2)}, u32[]{:S(2)}) collective-permute-start(bf16[256,768]{1,0:T(8,128)(2,1)S(1)} %collective-permute-done.7.xl), channel_id=1, source_target_pairs={{1,2},{2,3},{5,6},{6,7},{9,10},{10,11},{13,14},{14,15},{17,18},{18... | collective-permute-start | bytes 1179656 | tf_op jit(solution)/shard_map/ppermute | solution.py:609
  63.4 17.2 %collective-permute-start.14 = (bf16[256,768]{1,0:T(8,128)(2,1)}, bf16[256,768]{1,0:T(8,128)(2,1)S(1)}, u32[]{:S(2)}, u32[]{:S(2)}) collective-permute-start(bf16[256,768]{1,0:T(8,128)(2,1)} %collective-permute-done.12.xr), channel_id=1, source_target_pairs={{2,1},{1,0},{6,5},{5,4},{10,9},{9,8},{14,13},{13,12},{18,17},{17,1... | collective-permute-start | bytes 1179656 | tf_op jit(solution)/shard_map/ppermute | solution.py:609
  64.7 15.9 %collective-permute-start.13 = (bf16[256,768]{1,0:T(8,128)(2,1)}, bf16[256,768]{1,0:T(8,128)(2,1)S(1)}, u32[]{:S(2)}, u32[]{:S(2)}) collective-permute-start(bf16[256,768]{1,0:T(8,128)(2,1)} %collective-permute-done.11.xl), channel_id=1, source_target_pairs={{1,2},{2,3},{5,6},{6,7},{9,10},{10,11},{13,14},{14,15},{17,18},{18... | collective-permute-start | bytes 1179656 | tf_op jit(solution)/shard_map/ppermute | solution.py:609
  65.6 32.6 %collective-permute-start.6 = (bf16[256,768]{1,0:T(8,128)(2,1)}, bf16[256,768]{1,0:T(8,128)(2,1)S(1)}, u32[]{:S(2)}, u32[]{:S(2)}) collective-permute-start(bf16[256,768]{1,0:T(8,128)(2,1)} %collective-permute-done.4.xr), channel_id=1, source_target_pairs={{2,1},{1,0},{6,5},{5,4},{10,9},{9,8},{14,13},{13,12},{18,17},{17,1... | collective-permute-start | bytes 1179656 | tf_op jit(solution)/shard_map/ppermute | solution.py:609
  71.3 26.9 %collective-permute-start.5 = (bf16[256,768]{1,0:T(8,128)(2,1)}, bf16[256,768]{1,0:T(8,128)(2,1)S(1)}, u32[]{:S(2)}, u32[]{:S(2)}) collective-permute-start(bf16[256,768]{1,0:T(8,128)(2,1)} %collective-permute-done.3.xl), channel_id=1, source_target_pairs={{1,2},{2,3},{5,6},{6,7},{9,10},{10,11},{13,14},{14,15},{17,18},{18... | collective-permute-start | bytes 1179656 | tf_op jit(solution)/shard_map/ppermute | solution.py:609
  111.7 18.9 %copy-start.43 = (bf16[256,768]{1,0:T(8,128)(2,1)}, bf16[256,768]{1,0:T(8,128)(2,1)S(1)}, u32[]{:S(2)}) copy-start(bf16[256,768]{1,0:T(8,128)(2,1)S(1)} %get-tuple-element.69.attn.refs_9_) | copy-start | bytes 1179652
  120.1 11.3 %copy-start.32 = (bf16[1024,768]{1,0:T(8,128)(2,1)S(1)}, bf16[1024,768]{1,0:T(8,128)(2,1)}, u32[]{:S(2)}) copy-start(bf16[1024,768]{1,0:T(8,128)(2,1)} %copy-done.31) | copy-start | bytes 4718596
  120.1 11.3 %copy-start.35 = (bf16[1024,768]{1,0:T(8,128)(2,1)S(1)}, bf16[1024,768]{1,0:T(8,128)(2,1)}, u32[]{:S(2)}) copy-start(bf16[1024,768]{1,0:T(8,128)(2,1)} %copy-done.34) | copy-start | bytes 4718596
  131.3 19.6 %copy-start.4 = (bf16[3,256,768]{2,1,0:T(8,128)(2,1)S(1)}, bf16[3,256,768]{2,1,0:T(8,128)(2,1)}, u32[]{:S(2)}) copy-start(bf16[3,256,768]{2,1,0:T(8,128)(2,1)} %refs_15_.1) | copy-start | bytes 3538948
  131.4 19.6 %copy-start.41 = (bf16[256,768]{1,0:T(8,128)(2,1)S(1)}, bf16[256,768]{1,0:T(8,128)(2,1)}, u32[]{:S(2)}) copy-start(bf16[256,768]{1,0:T(8,128)(2,1)} %copy-done.40) | copy-start | bytes 1179652
  137.5 51.8 %collective-permute-start.16 = (bf16[256,896]{1,0:T(8,128)(2,1)S(1)}, bf16[256,896]{1,0:T(8,128)(2,1)S(1)}, u32[]{:S(2)}, u32[]{:S(2)}) collective-permute-start(bf16[256,896]{1,0:T(8,128)(2,1)S(1)} %get-tuple-element.87.grad.qf.g0), channel_id=1, source_target_pairs={{1,0},{2,1},{3,2},{5,4},{6,5},{7,6},{9,8},{10,9},{11,10},{13,12},{... | collective-permute-start | bytes 1376264 | tf_op jit(solution)/shard_map/ppermute | solution.py:609
  138.8 57.3 %collective-permute-start.15 = (bf16[256,896]{1,0:T(8,128)(2,1)S(1)}, bf16[256,896]{1,0:T(8,128)(2,1)S(1)}, u32[]{:S(2)}, u32[]{:S(2)}) collective-permute-start(bf16[256,896]{1,0:T(8,128)(2,1)S(1)} %get-tuple-element.87.grad.qf.g0), channel_id=1, source_target_pairs={{0,1},{1,2},{2,3},{4,5},{5,6},{6,7},{8,9},{9,10},{10,11},{12,13},{... | collective-permute-start | bytes 1376264 | tf_op jit(solution)/shard_map/ppermute | solution.py:609
  150.9 16.7 %copy-start.38 = (bf16[256,768]{1,0:T(8,128)(2,1)S(1)}, bf16[256,768]{1,0:T(8,128)(2,1)}, u32[]{:S(2)}) copy-start(bf16[256,768]{1,0:T(8,128)(2,1)} %copy-done.37) | copy-start | bytes 1179652
  161.4 16.7 %copy-start.49 = (bf16[256,768]{1,0:T(8,128)(2,1)}, bf16[256,768]{1,0:T(8,128)(2,1)S(1)}, u32[]{:S(2)}) copy-start(bf16[256,768]{1,0:T(8,128)(2,1)S(1)} %get-tuple-element.109.refs_8_) | copy-start | bytes 1179652
  161.4 16.7 %copy-start.51 = (bf16[256,768]{1,0:T(8,128)(2,1)}, bf16[256,768]{1,0:T(8,128)(2,1)S(1)}, u32[]{:S(2)}) copy-start(bf16[256,768]{1,0:T(8,128)(2,1)S(1)} %get-tuple-element.112.refs_14_) | copy-start | bytes 1179652
  161.4 35.9 %collective-permute-start.24 = (bf16[256,896]{1,0:T(8,128)(2,1)S(1)}, bf16[256,896]{1,0:T(8,128)(2,1)S(1)}, u32[]{:S(2)}, u32[]{:S(2)}) collective-permute-start(bf16[256,896]{1,0:T(8,128)(2,1)S(1)} %get-tuple-element.89.grad.qf.g0), channel_id=1, source_target_pairs={{1,0},{2,1},{3,2},{5,4},{6,5},{7,6},{9,8},{10,9},{11,10},{13,12},{... | collective-permute-start | bytes 1376264 | tf_op jit(solution)/shard_map/ppermute | solution.py:609
  162.7 41.5 %collective-permute-start.23 = (bf16[256,896]{1,0:T(8,128)(2,1)S(1)}, bf16[256,896]{1,0:T(8,128)(2,1)S(1)}, u32[]{:S(2)}, u32[]{:S(2)}) collective-permute-start(bf16[256,896]{1,0:T(8,128)(2,1)S(1)} %get-tuple-element.89.grad.qf.g0), channel_id=1, source_target_pairs={{0,1},{1,2},{2,3},{4,5},{5,6},{6,7},{8,9},{9,10},{10,11},{12,13},{... | collective-permute-start | bytes 1376264 | tf_op jit(solution)/shard_map/ppermute | solution.py:609
  178.9 26.6 %collective-permute-start.20 = (bf16[256,896]{1,0:T(8,128)(2,1)S(1)}, bf16[256,896]{1,0:T(8,128)(2,1)S(1)}, u32[]{:S(2)}, u32[]{:S(2)}) collective-permute-start(bf16[256,896]{1,0:T(8,128)(2,1)S(1)} %get-tuple-element.88.grad.qf.g0), channel_id=1, source_target_pairs={{1,0},{2,1},{3,2},{5,4},{6,5},{7,6},{9,8},{10,9},{11,10},{13,12},{... | collective-permute-start | bytes 1376264 | tf_op jit(solution)/shard_map/ppermute | solution.py:609
  183.4 14.8 %copy-start.17 = (bf16[1024,768]{1,0:T(8,128)(2,1)S(1)}, bf16[1024,768]{1,0:T(8,128)(2,1)}, u32[]{:S(2)}) copy-start(bf16[1024,768]{1,0:T(8,128)(2,1)} %copy-done.16) | copy-start | bytes 4718596
  183.4 14.9 %copy-start.19 = (bf16[1024,768]{1,0:T(8,128)(2,1)S(1)}, bf16[1024,768]{1,0:T(8,128)(2,1)}, u32[]{:S(2)}) copy-start(bf16[1024,768]{1,0:T(8,128)(2,1)} %copy-done.18) | copy-start | bytes 4718596
  183.4 14.9 %copy-start.21 = (bf16[1024,768]{1,0:T(8,128)(2,1)S(1)}, bf16[1024,768]{1,0:T(8,128)(2,1)}, u32[]{:S(2)}) copy-start(bf16[1024,768]{1,0:T(8,128)(2,1)} %copy-done.20) | copy-start | bytes 4718596
  189.3 16.9 %collective-permute-start.19 = (bf16[256,896]{1,0:T(8,128)(2,1)S(1)}, bf16[256,896]{1,0:T(8,128)(2,1)S(1)}, u32[]{:S(2)}, u32[]{:S(2)}) collective-permute-start(bf16[256,896]{1,0:T(8,128)(2,1)S(1)} %get-tuple-element.88.grad.qf.g0), channel_id=1, source_target_pairs={{0,1},{1,2},{2,3},{4,5},{5,6},{6,7},{8,9},{9,10},{10,11},{12,13},{... | collective-permute-start | bytes 1376264 | tf_op jit(solution)/shard_map/ppermute | solution.py:609
  196.0 13.2 %collective-permute-start.18 = (bf16[256,896]{1,0:T(8,128)(2,1)S(1)}, bf16[256,896]{1,0:T(8,128)(2,1)S(1)}, u32[]{:S(2)}, u32[]{:S(2)}) collective-permute-start(bf16[256,896]{1,0:T(8,128)(2,1)S(1)} %collective-permute-done.16.gr), channel_id=1, source_target_pairs={{2,1},{1,0},{6,5},{5,4},{10,9},{9,8},{14,13},{13,12},{18,17},{17,1... | collective-permute-start | bytes 1376264 | tf_op jit(solution)/shard_map/ppermute | solution.py:609
  197.3 12.5 %collective-permute-start.17 = (bf16[256,896]{1,0:T(8,128)(2,1)S(1)}, bf16[256,896]{1,0:T(8,128)(2,1)S(1)}, u32[]{:S(2)}, u32[]{:S(2)}) collective-permute-start(bf16[256,896]{1,0:T(8,128)(2,1)S(1)} %collective-permute-done.15.gl), channel_id=1, source_target_pairs={{1,2},{2,3},{5,6},{6,7},{9,10},{10,11},{13,14},{14,15},{17,18},{18... | collective-permute-start | bytes 1376264 | tf_op jit(solution)/shard_map/ppermute | solution.py:609
  198.3 11.6 %copy-start.30 = (bf16[1024,768]{1,0:T(8,128)(2,1)S(1)}, bf16[1024,768]{1,0:T(8,128)(2,1)}, u32[]{:S(2)}) copy-start(bf16[1024,768]{1,0:T(8,128)(2,1)} %copy-done.28) | copy-start | bytes 4718596
  198.3 11.6 %copy-start.33 = (bf16[1024,768]{1,0:T(8,128)(2,1)S(1)}, bf16[1024,768]{1,0:T(8,128)(2,1)}, u32[]{:S(2)}) copy-start(bf16[1024,768]{1,0:T(8,128)(2,1)} %copy-done.31) | copy-start | bytes 4718596
  198.3 11.6 %copy-start.36 = (bf16[1024,768]{1,0:T(8,128)(2,1)S(1)}, bf16[1024,768]{1,0:T(8,128)(2,1)}, u32[]{:S(2)}) copy-start(bf16[1024,768]{1,0:T(8,128)(2,1)} %copy-done.34) | copy-start | bytes 4718596
  204.2 14.3 %collective-permute-start.26 = (bf16[256,896]{1,0:T(8,128)(2,1)S(1)}, bf16[256,896]{1,0:T(8,128)(2,1)S(1)}, u32[]{:S(2)}, u32[]{:S(2)}) collective-permute-start(bf16[256,896]{1,0:T(8,128)(2,1)S(1)} %collective-permute-done.24.gr), channel_id=1, source_target_pairs={{2,1},{1,0},{6,5},{5,4},{10,9},{9,8},{14,13},{13,12},{18,17},{17,1... | collective-permute-start | bytes 1376264 | tf_op jit(solution)/shard_map/ppermute | solution.py:609
  205.5 13.0 %collective-permute-start.25 = (bf16[256,896]{1,0:T(8,128)(2,1)S(1)}, bf16[256,896]{1,0:T(8,128)(2,1)S(1)}, u32[]{:S(2)}, u32[]{:S(2)}) collective-permute-start(bf16[256,896]{1,0:T(8,128)(2,1)S(1)} %collective-permute-done.23.gl), channel_id=1, source_target_pairs={{1,2},{2,3},{5,6},{6,7},{9,10},{10,11},{13,14},{14,15},{17,18},{18... | collective-permute-start | bytes 1376264 | tf_op jit(solution)/shard_map/ppermute | solution.py:609
  206.2 22.1 %collective-permute-start.22 = (bf16[256,896]{1,0:T(8,128)(2,1)S(1)}, bf16[256,896]{1,0:T(8,128)(2,1)S(1)}, u32[]{:S(2)}, u32[]{:S(2)}) collective-permute-start(bf16[256,896]{1,0:T(8,128)(2,1)S(1)} %collective-permute-done.20.gr), channel_id=1, source_target_pairs={{2,1},{1,0},{6,5},{5,4},{10,9},{9,8},{14,13},{13,12},{18,17},{17,1... | collective-permute-start | bytes 1376264 | tf_op jit(solution)/shard_map/ppermute | solution.py:609
  209.2 19.1 %collective-permute-start.21 = (bf16[256,896]{1,0:T(8,128)(2,1)S(1)}, bf16[256,896]{1,0:T(8,128)(2,1)S(1)}, u32[]{:S(2)}, u32[]{:S(2)}) collective-permute-start(bf16[256,896]{1,0:T(8,128)(2,1)S(1)} %collective-permute-done.19.gl), channel_id=1, source_target_pairs={{1,2},{2,3},{5,6},{6,7},{9,10},{10,11},{13,14},{14,15},{17,18},{18... | collective-permute-start | bytes 1376264 | tf_op jit(solution)/shard_map/ppermute | solution.py:609
  253.3 149.4 %reduce-scatter.5.cloned.1.call-start = ((), (), s32[]{:S(2)}) async-start(), calls=%async_computation.3 | async-start | bytes 11943936 | tf_op jit(solution)/shard_map/reduce_scatter | solution.py:747
  290.1 192.0 %all-reduce.4.cloned.1.call-start = ((), (), s32[]{:S(2)}) async-start(), calls=%async_computation.6 | async-start | bytes 3588096 | tf_op jit(solution)/shard_map/psum | solution.py:748
  (46 other events, 140.4 us)
Sparse Core Ops, SparseCore 0:
  15.5 37.4 all-gather.4
  54.9 63.8 all-gather.6
  253.4 63.2 reduce-scatter.2
  320.5 82.1 reduce-scatter.4
  405.2 76.8 all-reduce.3
